TPU v7x, 32 devices: a whole 2x2x4 slice. The times are simulated.
32 devices in a mesh: section: 2 (over x), patch: 4 (over z), fsdp: 4 (over y, core).
Axes of the slice: x: 2, y: 2, z: 4, core: 2. Of those that a mesh axis runs over, the one named last changes fastest.
Arguments:
- latent: float32 [8, 4, 256, 64], P('fsdp', 'patch', 'section'), may hold values from -60 to 60
- counts: int32 [8, 4], P('fsdp'), may hold values from 64 to 256, as said below
- steps_idx: int32 [8], P('fsdp'), may hold values from 0 to 49
- embed_weight: bfloat16 [64, 1536], replicated, may hold values from -0.75 to 0.75
- wqkv: bfloat16 [2, 1536, 4608], P('section', 'fsdp'), may hold values from -0.15625 to 0.15625
- wo: bfloat16 [2, 1536, 1536], P('section', 'fsdp'), may hold values from -0.15625 to 0.15625
- qk_gain: float32 [2, 3072], P('section'), may hold values from 0.1 to 1.9
- modulation: float32 [2, 50, 4608], P('section'), may hold values from -3 to 3
- head_mod: float32 [50, 3072], replicated, may hold values from -3 to 3
- head_weight: bfloat16 [1536, 64], replicated, may hold values from -0.15625 to 0.15625
- stale_cache: bfloat16 [2, 8, 4, 256, 3072], P('section', 'fsdp', 'patch'), may hold values from -210 to 210
Outputs:
- velocity: float32 [8, 4, 256, 64], P('fsdp', 'patch', 'section')
- new_latent: float32 [8, 4, 256, 64], P('fsdp', 'patch', 'section')
- cache_out: bfloat16 [2, 8, 4, 256, 3072], P('section', 'fsdp', 'patch')
Inputs may be any that keep to these rules, and one draw needn't show every extreme that they name: `counts`: in every video one patch holds exactly 256 tokens.
All inputs are finite; a program needn't handle non-finite values.
Results may differ from a plain program's by a relative error of at most 0.0071.
Values may be sent and summed in bfloat16 or wider, within the bound.
A program may use at most 192 MiB of HBM per device.

v0:
```python
import math

import jax
import jax.numpy as jnp
from jax import lax
from jax.sharding import PartitionSpec as P

HEADS = 12
HD = 128
TSTEPS = 50


EPS = 1e-06


def shifted(shard, axis, by):
    devices = lax.axis_size(axis)
    pairs = [(i, i + by) for i in range(devices) if 0 <= i + by < devices]
    return lax.ppermute(shard, axis, pairs)


def layer_norm(hidden):
    center = hidden - jnp.mean(hidden, axis=-1, keepdims=True)
    return center * lax.rsqrt(jnp.mean(center * center, axis=-1, keepdims=True) + EPS)


def rms_norm(values_in, gain_vec):
    return (
        values_in
        * lax.rsqrt(jnp.mean(values_in * values_in, axis=-1, keepdims=True) + EPS)
        * gain_vec
    )


def sigma_of(step_float):
    remain = 1.0 - step_float / TSTEPS
    return 5.0 * remain / (1.0 + 4.0 * remain)


def dense_attend(queries, key_rows, value_rows, key_live):
    groups, query_count = (queries.shape[0], queries.shape[1])
    query_heads = queries.reshape(groups, query_count, HEADS, HD)
    key_heads = key_rows.reshape(groups, key_rows.shape[1], HEADS, HD)
    value_heads = value_rows.reshape(groups, value_rows.shape[1], HEADS, HD)
    scores = jnp.einsum(
        "gqhd,gkhd->ghqk", query_heads, key_heads, preferred_element_type=jnp.float32
    ) / math.sqrt(HD)
    scores = jnp.where(key_live[:, None, None, :], scores, -jnp.inf)
    top_score = jnp.max(scores, axis=-1, keepdims=True)
    exp_scores = jnp.exp(scores - top_score)
    denom_sum = jnp.sum(exp_scores, axis=-1)
    mixed_out = jnp.einsum(
        "ghqk,gkhd->gqhd",
        exp_scores.astype(jnp.bfloat16),
        value_heads,
        preferred_element_type=jnp.float32,
    )
    mixed_out = mixed_out / jnp.transpose(denom_sum, (0, 2, 1))[..., None]
    return mixed_out.reshape(groups, query_count, HEADS * HD).astype(jnp.bfloat16)


def run_layer(hidden, modulation_rows, project_in, project_out, gain_rows, attend_fn):
    groups, slot_count, model_width = hidden.shape
    shift_vec = modulation_rows[:, None, :model_width]
    scale_vec = modulation_rows[:, None, model_width : 2 * model_width]
    gate_vec = modulation_rows[:, None, 2 * model_width :]
    normed = (layer_norm(hidden) * (1.0 + scale_vec) + shift_vec).astype(jnp.bfloat16)
    projected = project_in(normed.reshape(-1, model_width))
    projected = projected.reshape(groups, slot_count, 3 * model_width)
    queries = rms_norm(projected[..., :model_width], gain_rows[:model_width]).astype(jnp.bfloat16)
    fresh_keys = rms_norm(
        projected[..., model_width : 2 * model_width], gain_rows[model_width:]
    ).astype(jnp.bfloat16)
    fresh_values = projected[..., 2 * model_width :].astype(jnp.bfloat16)
    fresh_kv = jnp.concatenate([fresh_keys, fresh_values], axis=-1)
    attended = attend_fn(queries, fresh_kv)
    update = project_out(attended.reshape(-1, model_width))
    return (hidden + gate_vec * update.reshape(groups, slot_count, model_width), fresh_kv)


def body(
    latent,
    counts,
    steps_idx,
    embed_weight,
    wqkv,
    wo,
    qk_gain,
    modulation,
    head_mod,
    head_weight,
    stale_cache,
):
    section_index = lax.axis_index("section")
    own_patch = lax.axis_index("patch")
    first_section = section_index == 0
    videos = latent.shape[0]
    patch_rows = stale_cache.shape[3]
    model_width = embed_weight.shape[1]
    patch_count = counts.shape[1]
    zero_index = jnp.zeros((), jnp.int32)
    proj_full, out_full = (
        lax.all_gather(wqkv, "fsdp", axis=1, tiled=True),
        lax.all_gather(wo, "fsdp", axis=1, tiled=True),
    )
    proj_full = proj_full[0]
    out_full = out_full[0]

    def project_in(left):
        return jnp.dot(left, proj_full, preferred_element_type=jnp.float32)

    def project_out(left):
        return jnp.dot(left, out_full, preferred_element_type=jnp.float32)

    rows_full = lax.all_gather(latent.astype(jnp.bfloat16), "section", axis=2, tiled=True)
    start_hidden = jnp.dot(
        rows_full.reshape(-1, rows_full.shape[3]), embed_weight, preferred_element_type=jnp.float32
    )
    start_hidden = start_hidden.reshape(videos, patch_rows, model_width)
    step_onehot = (jnp.arange(TSTEPS, dtype=jnp.int32)[None, :] == steps_idx[:, None]).astype(
        jnp.float32
    )
    modulation_all = jnp.dot(step_onehot, modulation[0], precision=lax.Precision.HIGHEST)
    head_rows = jnp.dot(step_onehot, head_mod, precision=lax.Precision.HIGHEST)
    gain_rows = qk_gain[0]
    slot_iota = jnp.arange(patch_rows, dtype=jnp.int32)
    own_count = jnp.sum(
        jnp.where(jnp.arange(patch_count, dtype=jnp.int32)[None, :] == own_patch, counts, 0), axis=1
    )
    own_live = slot_iota[None, :] < own_count[:, None]
    key_live_all = (slot_iota[None, None, :] < counts[:, :, None]).reshape(
        videos, patch_count * patch_rows
    )
    stale_all = lax.all_gather(stale_cache, "patch", axis=2, tiled=True)[0].reshape(
        videos, patch_count * patch_rows, 2 * model_width
    )
    group_size = videos // videos
    received = jnp.zeros((group_size, patch_rows, model_width), jnp.float32)
    hidden_end = jnp.zeros((videos, patch_rows, model_width), jnp.float32)
    cache_buf = jnp.zeros((videos, patch_rows, 2 * model_width), jnp.bfloat16)
    for tick_index in range(videos + 1):
        group_index = jnp.clip(
            jnp.where(first_section, tick_index, tick_index - 1), 0, videos - 1
        ).astype(jnp.int32)
        first_video = group_index * group_size
        source_group = min(tick_index, videos - 1)
        source_zero = start_hidden[source_group * group_size : (source_group + 1) * group_size]
        hidden_in = jnp.where(first_section, source_zero, received)
        modulation_group = lax.dynamic_slice_in_dim(modulation_all, first_video, group_size, 0)
        stale_group = lax.dynamic_slice_in_dim(stale_all, first_video, group_size, 0)
        live_group = lax.dynamic_slice_in_dim(key_live_all, first_video, group_size, 0)

        def attend_fn(queries, fresh_kv, stale_group=stale_group, live_group=live_group):
            seen_rows = lax.dynamic_update_slice(
                stale_group, fresh_kv, (zero_index, own_patch * patch_rows, zero_index)
            )
            return dense_attend(
                queries, seen_rows[..., :model_width], seen_rows[..., model_width:], live_group
            )

        hidden_out, fresh_kv = run_layer(
            hidden_in, modulation_group, project_in, project_out, gain_rows, attend_fn
        )
        own_group = lax.dynamic_slice_in_dim(own_live, first_video, group_size, 0)
        fresh_kv = jnp.where(own_group[..., None], fresh_kv, jnp.zeros_like(fresh_kv))
        is_valid = jnp.where(first_section, tick_index < videos, tick_index >= 1)
        cache_buf = jnp.where(
            is_valid,
            lax.dynamic_update_slice(cache_buf, fresh_kv, (first_video, zero_index, zero_index)),
            cache_buf,
        )
        hidden_end = jnp.where(
            is_valid,
            lax.dynamic_update_slice(hidden_end, hidden_out, (first_video, zero_index, zero_index)),
            hidden_end,
        )
        if tick_index < videos:
            received = shifted(hidden_out.astype(jnp.bfloat16), "section", 1).astype(jnp.float32)
    head_in = (
        layer_norm(hidden_end) * (1.0 + head_rows[:, None, model_width:])
        + head_rows[:, None, :model_width]
    ).astype(jnp.bfloat16)
    velocity = jnp.dot(
        head_in.reshape(-1, model_width), head_weight, preferred_element_type=jnp.float32
    )
    velocity = velocity.reshape(videos, patch_rows, head_weight.shape[1])
    velocity = jnp.where(own_live[..., None], velocity, jnp.zeros_like(velocity))
    half_rows = patch_rows // 2
    returned = shifted(velocity[:, :half_rows].astype(jnp.bfloat16), "section", -1).astype(
        jnp.float32
    )
    mine_half = jnp.where(first_section, returned, velocity[:, half_rows:])
    step_float = steps_idx.astype(jnp.float32)
    step_delta = sigma_of(step_float + 1.0) - sigma_of(step_float)
    new_latent = latent + step_delta[:, None, None, None] * mine_half[:, None]
    return (mine_half[:, None], new_latent, cache_buf[None, :, None])


def solution(mesh):
    in_specs = (
        P("fsdp", "patch", "section", None),
        P("fsdp", None),
        P("fsdp"),
        P(),
        P("section", "fsdp", None),
        P("section", "fsdp", None),
        P("section", None),
        P("section", None, None),
        P(),
        P(),
        P("section", "fsdp", "patch", None, None),
    )
    out_specs = (
        P("fsdp", "patch", "section", None),
        P("fsdp", "patch", "section", None),
        P("section", "fsdp", "patch", None, None),
    )
    return jax.shard_map(body, mesh=mesh, in_specs=in_specs, out_specs=out_specs, check_vma=False)
```

profile of v0, /device:TPU:0, one launch (start us, length us, event | category | flops | bytes accessed | tf_op | source)
XLA Modules:
  0.0 515.1 jit_solution(11341558818491198296)
XLA Ops:
  9.5 5.5 %all_gather.12 = bf16[2,1,256,64]{2,3,1,0:T(8,128)(2,1)S(1)} all-gather(bf16[2,1,128,64]{2,3,1,0:T(8,128)(2,1)S(1)} %convert_element_type.99), channel_id=1, replica_groups=mesh['section'=2,'patch'=4,'fsdp'=4] {'section'}, dimensions={2}, use_global_device_ids=true | all-gather | bytes 98304 | tf_op jit(solution)/shard_map/all_gather | solution.py:115
  18.8 211.8 %all-gather.4.cloned.1.call-done = bf16[1,2,4,256,3072]{4,3,2,1,0:T(8,128)(2,1)} async-done(((bf16[1,2,1,256,3072]{4,3,2,1,0:T(8,128)(2,1)}), bf16[1,2,4,256,3072]{4,3,2,1,0:T(8,128)(2,1)}) %all-gather.4.cloned.1.call-update) | async-done | bytes 12582928 | tf_op jit(solution)/shard_map/all_gather | solution.py:134
  230.6 16.0 %constant_dynamic-slice_fusion.3 = (bf16[1,1024,3072]{2,1,0:T(8,128)(2,1)}, bf16[1,1024,3072]{2,1,0:T(8,128)(2,1)}, bf16[1,1024,3072]{2,1,0:T(8,128)(2,1)}) fusion(bf16[2,1024,3072]{2,1,0:T(8,128)(2,1)} %bitcast.193, s32[]{:T(128)S(6)} %min.12, s32[]{:T(128)S(6)} %min.11, s32[]{:T(128)S(6)} %min.10), kind=kLoop, calls=%fused_computation.146 | loop fusion | bytes 37748748 | tf_op jit(solution)/shard_map/dynamic_slice | solution.py:150
  246.6 8.7 %copy.54 = bf16[1,1024,3072]{1,2,0:T(8,128)(2,1)} copy(bf16[1,1024,3072]{2,1,0:T(8,128)(2,1)} %get-tuple-element.34) | data formatting | bytes 12582912
  255.3 66.1 %all-gather.6.cloned.1.call-done = bf16[1,1536,4608]{2,1,0:T(8,128)(2,1)} async-done(((bf16[1,384,4608]{2,1,0:T(8,128)(2,1)}), bf16[1,1536,4608]{2,1,0:T(8,128)(2,1)}) %all-gather.6.cloned.1.call-update) | async-done | bytes 14155792 | tf_op jit(solution)/shard_map/all_gather | solution.py:103
  321.4 7.8 %fusion.15 = f32[1,256,4608]{2,1,0:T(8,128)S(1)} fusion(bf16[1,1536,4608]{2,1,0:T(8,128)(2,1)} %all-gather.6.cloned.1.call-done, f32[512,1536]{1,0:T(8,128)} %copy-done.1, f32[1536]{0:T(1024)S(1)} %get-tuple-element.23, f32[1536]{0:T(1024)S(1)} %get-tuple-element.19, f32[256]{0:T(256)S(1)} %add_rsqrt_fusion.9, f32[256]{0:T(256)S(1)} %broadcast_multiply_fusion.3, ...), kind=kOutput, calls=%fused_computation.21 | convolution fusion | flops 3626237952 | bytes 20461568 | tf_op jit(solution)/shard_map/dot_general | solution.py:110
  329.9 2.1 broadcast_in_dim.155
  332.0 1.8 select_dynamic-update-slice_fusion.1
  335.6 2.7 constant_dynamic-update-slice_fusion.3
  338.3 3.6 fusion.134
  341.9 2.0 fusion.6
  343.9 3.0 fusion.9
  347.0 3.3 fusion.80
  350.3 10.2 %all-gather.8.cloned.1.call-done = bf16[1,1536,1536]{2,1,0:T(8,128)(2,1)} async-done(((bf16[1,384,1536]{2,1,0:T(8,128)(2,1)}), bf16[1,1536,1536]{2,1,0:T(8,128)(2,1)}) %all-gather.8.cloned.1.call-update) | async-done | bytes 4718608 | tf_op jit(solution)/shard_map/all_gather | solution.py:104
  360.4 2.0 broadcast_in_dim.85
  363.5 4.9 bitcast_dynamic-update-slice_fusion.1
  368.4 3.4 collective-permute-start
  371.8 9.0 %copy.55 = bf16[1,1024,3072]{1,2,0:T(8,128)(2,1)} copy(bf16[1,1024,3072]{2,1,0:T(8,128)(2,1)} %get-tuple-element.33) | data formatting | bytes 12582912
  380.8 8.2 %collective-permute-done = bf16[1,256,1536]{2,1,0:T(8,128)(2,1)S(1)} collective-permute-done((bf16[1,256,1536]{2,1,0:T(8,128)(2,1)S(1)}, bf16[1,256,1536]{2,1,0:T(8,128)(2,1)S(1)}, u32[]{:S(2)}, u32[]{:S(2)}) %collective-permute-start) | collective-permute-done | bytes 786464 | tf_op jit(solution)/shard_map/ppermute | solution.py:19
  389.0 1.6 fusion.130
  390.6 1.8 multiply_reduce_fusion.6
  392.4 7.5 %fusion.18 = f32[1,256,4608]{2,1,0:T(8,128)S(1)} fusion(bf16[1,1536,4608]{2,1,0:T(8,128)(2,1)} %all-gather.6.cloned.1.call-done, f32[1536]{0:T(1024)S(1)} %get-tuple-element.22, f32[1536]{0:T(1024)S(1)} %get-tuple-element.17, f32[256]{0:T(256)S(1)} %add_rsqrt_fusion.6, f32[256]{0:T(256)S(1)} %broadcast_multiply_fusion.2, ...), kind=kOutput, calls=%fused_computation.22 | convolution fusion | flops 3626631168 | bytes 21252096 | tf_op jit(solution)/shard_map/dot_general | solution.py:110
  401.5 1.8 select_dynamic-update-slice_fusion
  403.3 1.6 copy.33
  404.9 2.7 constant_dynamic-update-slice_fusion.2
  407.6 6.3 %fusion.133 = (bf16[1,1024,1536]{1,2,0:T(8,128)(2,1)}, bf16[1,1024,1536]{1,2,0:T(8,128)(2,1)}) fusion(bf16[1,1024,3072]{1,2,0:T(8,128)(2,1)} %constant_dynamic-update-slice_fusion.2), kind=kLoop, calls=%fused_computation.190 | loop fusion | bytes 12582912 | tf_op jit(solution)/shard_map/slice | solution.py:158
  414.2 3.9 fusion.7
  418.1 3.0 fusion.11
  421.2 4.7 fusion.79
  425.9 4.9 fusion.135
  430.9 4.4 collective-permute-start.1
  435.6 8.8 %copy.56 = bf16[1,1024,3072]{1,2,0:T(8,128)(2,1)} copy(bf16[1,1024,3072]{2,1,0:T(8,128)(2,1)} %get-tuple-element.32) | data formatting | bytes 12582912
  444.4 3.9 copy.72
  448.4 3.2 collective-permute-done.1
  452.2 7.5 %fusion.21 = f32[1,256,4608]{2,1,0:T(8,128)S(1)} fusion(bf16[1,1536,4608]{2,1,0:T(8,128)(2,1)} %all-gather.6.cloned.1.call-done, f32[1536]{0:T(1024)S(1)} %get-tuple-element.21, f32[1536]{0:T(1024)S(1)} %get-tuple-element.16, f32[256]{0:T(256)S(1)} %add_rsqrt_fusion.3, f32[256]{0:T(256)S(1)} %broadcast_multiply_fusion.1, ...), kind=kOutput, calls=%fused_computation.23 | convolution fusion | flops 3626631168 | bytes 21252096 | tf_op jit(solution)/shard_map/dot_general | solution.py:110
  462.6 2.6 copy.37
  465.2 2.7 constant_dynamic-update-slice_fusion
  467.9 6.2 %fusion.132 = (bf16[1,1024,1536]{1,2,0:T(8,128)(2,1)}, bf16[1,1024,1536]{1,2,0:T(8,128)(2,1)}) fusion(bf16[1,1024,3072]{1,2,0:T(8,128)(2,1)} %constant_dynamic-update-slice_fusion), kind=kLoop, calls=%fused_computation.189 | loop fusion | bytes 12582912 | tf_op jit(solution)/shard_map/slice | solution.py:158
  474.1 2.3 copy.38
  476.4 4.2 fusion.8
  480.6 3.0 fusion.13
  483.6 4.7 fusion.78
  488.4 5.5 %fusion.72 = f32[2,256,1536]{2,1,0:T(8,128)} fusion(f32[2,256,1536]{2,1,0:T(8,128)} %get-tuple-element.52, s32[]{:T(128)S(6)} %min.12, bf16[256,1536]{0,1:T(8,128)(2,1)S(1)} %bitcast.204, bf16[1,1536,1536]{2,1,0:T(8,128)(2,1)} %all-gather.8.cloned.1.call-done, f32[1536]{0:T(1024)S(1)} %get-tuple-element.15, pred[]{:T(512)S(6)} %select_n.179, ...), kind=kOutput, calls=%fused_computation.55 | convolution fusion | flops 1209925632 | bytes 11016198 | tf_op jit(solution)/shard_map/dot_general | solution.py:113
  493.9 2.2 reduce_sum.187
  496.0 2.5 multiply_reduce_fusion
  498.6 2.7 fusion.88
  502.6 2.3 bitcast_dynamic-update-slice_fusion
  504.9 2.2 collective-permute-done.2
  (94 shorter events, 17.8 us)
Async XLA Ops:
  7.2 428.1 %copy-start = (f32[50,3072]{1,0:T(8,128)S(1)}, f32[50,3072]{1,0:T(8,128)}, u32[]{:S(2)}) copy-start(f32[50,3072]{1,0:T(8,128)} %param.19) | copy-start | bytes 1843204
  7.2 223.4 %all-gather.4.cloned.1.call-start = ((), (), s32[]{:S(2)}) async-start(), calls=%async_computation | async-start | bytes 15728640 | tf_op jit(solution)/shard_map/all_gather | solution.py:134
  7.9 1.5 copy-start.11
  7.9 7.2 %copy-start.12 = (bf16[64,1536]{1,0:T(8,128)(2,1)S(1)}, bf16[64,1536]{1,0:T(8,128)(2,1)}, u32[]{:S(2)}) copy-start(bf16[64,1536]{1,0:T(8,128)(2,1)} %param.14) | copy-start | bytes 589828
  7.9 313.4 %all-gather.6.cloned.1.call-start = ((), (), s32[]{:S(2)}) async-start(), calls=%async_computation.1 | async-start | bytes 17694720 | tf_op jit(solution)/shard_map/all_gather | solution.py:103
  8.7 351.8 %all-gather.8.cloned.1.call-start = ((), (), s32[]{:S(2)}) async-start(), calls=%async_computation.2 | async-start | bytes 5898240 | tf_op jit(solution)/shard_map/all_gather | solution.py:104
  15.1 2.6 copy-start.13
  15.1 2.7 copy-start.14
  15.1 3.0 copy-start.10
  15.1 3.0 copy-start.15
  15.7 1.6 copy-start.1
  360.4 3.0 copy-start.2
  368.4 20.6 %collective-permute-start = (bf16[1,256,1536]{2,1,0:T(8,128)(2,1)S(1)}, bf16[1,256,1536]{2,1,0:T(8,128)(2,1)S(1)}, u32[]{:S(2)}, u32[]{:S(2)}) collective-permute-start(bf16[1,256,1536]{2,1,0:T(8,128)(2,1)S(1)} %bitcast.213), channel_id=1, source_target_pairs={{0,16},{1,17},{2,18},{3,19},{4,20},{5,21},{6,22},{7,23},{8,24},{9,... | collective-permute-start | bytes 2359304 | tf_op jit(solution)/shard_map/ppermute | solution.py:19
  380.8 11.6 %copy-start.3 = (f32[512,1536]{1,0:T(8,128)S(1)}, f32[512,1536]{1,0:T(8,128)}, u32[]{:S(2)}) copy-start(f32[512,1536]{1,0:T(8,128)} %copy-done.1) | copy-start | bytes 9437188
  407.6 6.3 %copy-start.9 = (bf16[1,256,1536]{2,1,0:T(8,128)(2,1)S(1)}, bf16[1,256,1536]{2,1,0:T(8,128)(2,1)}, u32[]{:S(2)}) copy-start(bf16[1,256,1536]{2,1,0:T(8,128)(2,1)} %get-tuple-element.43) | copy-start | bytes 2359300
  421.1 4.8 copy-start.4
  430.9 20.7 %collective-permute-start.1 = (bf16[1,256,1536]{2,1,0:T(8,128)(2,1)S(1)}, bf16[1,256,1536]{2,1,0:T(8,128)(2,1)S(1)}, u32[]{:S(2)}, u32[]{:S(2)}) collective-permute-start(bf16[1,256,1536]{2,1,0:T(8,128)(2,1)S(1)} %get-tuple-element.51), channel_id=1, source_target_pairs={{0,16},{1,17},{2,18},{3,19},{4,20},{5,21},{6,22},{7,23},{8,24},{9,... | collective-permute-start | bytes 2359304 | tf_op jit(solution)/shard_map/ppermute | solution.py:19
  444.4 7.1 %copy-start.5 = (f32[512,1536]{1,0:T(8,128)S(1)}, f32[512,1536]{1,0:T(8,128)}, u32[]{:S(2)}) copy-start(f32[512,1536]{1,0:T(8,128)} %copy-done.1) | copy-start | bytes 9437188
  483.6 4.8 copy-start.6
  493.9 4.7 copy-start.16
  496.0 6.5 %copy-start.7 = (bf16[1,2,1,256,3072]{4,3,1,2,0:T(8,128)(2,1)S(1)}, bf16[1,2,1,256,3072]{4,3,1,2,0:T(8,128)(2,1)}, u32[]{:S(2)}) copy-start(bf16[1,2,1,256,3072]{4,3,1,2,0:T(8,128)(2,1)} %copy.72) | copy-start | bytes 9437188
  501.2 5.8 %collective-permute-start.2 = (bf16[2,128,64]{1,2,0:T(8,128)(2,1)S(1)}, bf16[2,128,64]{1,2,0:T(8,128)(2,1)S(1)}, u32[]{:S(2)}, u32[]{:S(2)}) collective-permute-start(bf16[2,128,64]{1,2,0:T(8,128)(2,1)S(1)} %slice.225), channel_id=1, source_target_pairs={{16,0},{17,1},{18,2},{19,3},{20,4},{21,5},{22,6},{23,7},{24,8},{25... | collective-permute-start | bytes 98312 | tf_op jit(solution)/shard_map/ppermute | solution.py:19
  504.9 3.5 copy-start.8
Sparse Core Ops, SparseCore 0:
  9.6 220.9 all-gather.3
  232.1 89.2 all-gather.5
  322.9 37.4 all-gather.7
where the time goes:
time: 526 us; the launch traced here: 515 us
  waiting for transfers between devices  304 us (58%)
  local copies, waits for them, and re-layouts  86.2 us (16%)
  matrix products  65.1 us (12%)
  other arithmetic  30.9 us (6%)
  between operations  14.4 us (3%)
  starting transfers between devices  9.2 us (2%)
  blocking collectives  5.51 us (1%)
    all_gather x1, waiting for transfers between devices, body(): lax.all_gather(stale_cache, 'patch', axis=2, tiled=True)[0]  212 us
    all_gather x1, waiting for transfers between devices, body(): lax.all_gather(wqkv, 'fsdp', axis=1, tiled=True)  66.1 us
    unnamed x43, local copies, waits for them, and re-layouts  33 us
    dot_general x3, matrix products, project_in(): return jnp.dot(left, proj_full, preferred_element_type=jnp.float32)  22.8 us
    slice x3, local copies, waits for them, and re-layouts, attend_fn(): seen_rows[..., :model_width]  16 us
    dynamic_slice x1, local copies, waits for them, and re-layouts, body(): lax.dynamic_slice_in_dim(stale_all, first_video, group_size, 0)  16 us
    dot_general x3, matrix products, project_out(): return jnp.dot(left, out_full, preferred_element_type=jnp.float32)  15.3 us
    ppermute x3, waiting for transfers between devices, shifted(): return lax.ppermute(shard, axis, pairs)  13.5 us
  transfers between devices with their start and end apart: 6, of which 6 were waited for; matrix products, arithmetic and copies ran while one was open for 16% of the time, Pallas kernels for 0%

commit v1 on v0

v1 whole, which is shorter than its diff:
```python
import math

import jax
import jax.numpy as jnp
from jax import lax
from jax.experimental import pallas as pl
from jax.experimental.pallas import tpu as pltpu
from jax.sharding import PartitionSpec as P

HEADS = 12
HD = 128
TSTEPS = 50


EPS = 1e-06


def shifted(shard, axis, by):
    devices = lax.axis_size(axis)
    pairs = [(i, i + by) for i in range(devices) if 0 <= i + by < devices]
    return lax.ppermute(shard, axis, pairs)


def layer_norm(hidden):
    center = hidden - jnp.mean(hidden, axis=-1, keepdims=True)
    return center * lax.rsqrt(jnp.mean(center * center, axis=-1, keepdims=True) + EPS)


def rms_norm(values_in, gain_vec):
    return (
        values_in
        * lax.rsqrt(jnp.mean(values_in * values_in, axis=-1, keepdims=True) + EPS)
        * gain_vec
    )


def sigma_of(step_float):
    remain = 1.0 - step_float / TSTEPS
    return 5.0 * remain / (1.0 + 4.0 * remain)


HEADS_STEP = 2


def attend_kernel(counts_ref, q_ref, *refs):
    blocks = (len(refs) - 1) // 2
    out_ref = refs[-1]
    for head in range(q_ref.shape[1] // HD):
        cols = slice(head * HD, (head + 1) * HD)
        query = q_ref[:, cols]
        scores = []
        for b in range(blocks):
            score = lax.dot_general(
                query, refs[2 * b][:, cols], (((1,), (1,)), ((), ())), preferred_element_type=jnp.float32
            ) * (1.0 / math.sqrt(HD))
            slot = lax.broadcasted_iota(jnp.int32, score.shape, 1)
            scores.append(jnp.where(slot < counts_ref[b], score, -jnp.inf))
        top = scores[0]
        for score in scores[1:]:
            top = jnp.maximum(top, score)
        top = jnp.max(top, axis=1, keepdims=True)
        total = None
        mixed = None
        for b in range(blocks):
            weight = jnp.exp(scores[b] - top)
            part = jnp.dot(
                weight.astype(jnp.bfloat16), refs[2 * b + 1][:, cols], preferred_element_type=jnp.float32
            )
            total = weight if total is None else total + weight
            mixed = part if mixed is None else mixed + part
        denom = jnp.sum(total, axis=1, keepdims=True)
        out_ref[:, cols] = (mixed / denom).astype(jnp.bfloat16)


def attend(queries, kv_blocks, block_counts):
    rows, model_width = queries.shape
    cols = HEADS_STEP * HD
    steps = model_width // cols
    specs = [pl.BlockSpec(memory_space=pltpu.SMEM), pl.BlockSpec((rows, cols), lambda h: (0, h))]
    operands = [block_counts, queries]
    for kv in kv_blocks:
        specs.append(pl.BlockSpec((kv.shape[0], cols), lambda h: (0, h)))
        specs.append(pl.BlockSpec((kv.shape[0], cols), lambda h: (0, h + steps)))
        operands += [kv, kv]
    keys = sum(kv.shape[0] for kv in kv_blocks)
    return pl.pallas_call(
        attend_kernel,
        grid=(steps,),
        in_specs=specs,
        out_specs=pl.BlockSpec((rows, cols), lambda h: (0, h)),
        out_shape=jax.ShapeDtypeStruct((rows, model_width), jnp.bfloat16),
        cost_estimate=pl.CostEstimate(
            flops=4 * rows * keys * model_width,
            bytes_accessed=4 * (rows + keys) * model_width,
            transcendentals=rows * keys * HEADS,
        ),
    )(*operands)


def body(
    latent,
    counts,
    steps_idx,
    embed_weight,
    wqkv,
    wo,
    qk_gain,
    modulation,
    head_mod,
    head_weight,
    stale_cache,
):
    section_index = lax.axis_index("section")
    own_patch = lax.axis_index("patch")
    first_section = section_index == 0
    videos = latent.shape[0]
    assert videos == 2 and lax.axis_size("section") == 2
    patch_rows = stale_cache.shape[3]
    model_width = embed_weight.shape[1]
    patch_count = counts.shape[1]
    early = section_index
    late = 1 - section_index
    rows_full = lax.all_gather(latent.astype(jnp.bfloat16), "section", axis=2, tiled=True)
    proj_full = lax.all_gather(wqkv[0], "fsdp", axis=0, tiled=True)
    out_full = lax.all_gather(wo[0], "fsdp", axis=0, tiled=True)
    ring = [(i, (i + 1) % patch_count) for i in range(patch_count)]

    def around(video, after=None):
        block = lax.dynamic_index_in_dim(stale_cache[0, :, 0], video, 0, keepdims=False)
        if after is not None:
            block, _ = lax.optimization_barrier((block, after))
        blocks = []
        for _ in range(patch_count - 1):
            block = lax.ppermute(block, "patch", ring)
            blocks.append(block)
        return blocks

    early_blocks = around(early)
    late_blocks = around(late, early_blocks[-1])

    start_hidden = jnp.dot(
        rows_full.reshape(-1, rows_full.shape[3]), embed_weight, preferred_element_type=jnp.float32
    )
    start_hidden = start_hidden.reshape(videos, patch_rows, model_width)
    step_onehot = (jnp.arange(TSTEPS, dtype=jnp.int32)[None, :] == steps_idx[:, None]).astype(
        jnp.float32
    )
    modulation_all = jnp.dot(step_onehot, modulation[0], precision=lax.Precision.HIGHEST)
    head_rows = jnp.dot(step_onehot, head_mod, precision=lax.Precision.HIGHEST)
    gain_rows = qk_gain[0]
    slot_iota = jnp.arange(patch_rows, dtype=jnp.int32)
    ring_counts = jnp.stack(
        [jnp.take(counts, (own_patch - k) % patch_count, axis=1) for k in range(patch_count)], axis=1
    )
    own_live = slot_iota[None, :] < ring_counts[:, :1]

    def layer(hidden, video, stale_blocks):
        mod = lax.dynamic_index_in_dim(modulation_all, video, 0)
        block_counts = lax.dynamic_index_in_dim(ring_counts, video, 0, keepdims=False)
        shift_vec = mod[:, :model_width]
        scale_vec = mod[:, model_width : 2 * model_width]
        gate_vec = mod[:, 2 * model_width :]
        normed = (layer_norm(hidden) * (1.0 + scale_vec) + shift_vec).astype(jnp.bfloat16)
        projected = jnp.dot(normed, proj_full, preferred_element_type=jnp.float32)
        queries = rms_norm(projected[:, :model_width], gain_rows[:model_width]).astype(jnp.bfloat16)
        keys = rms_norm(projected[:, model_width : 2 * model_width], gain_rows[model_width:])
        fresh_kv = jnp.concatenate(
            [keys.astype(jnp.bfloat16), projected[:, 2 * model_width :].astype(jnp.bfloat16)], axis=-1
        )
        attended = attend(queries, [fresh_kv] + stale_blocks, block_counts)
        update = jnp.dot(attended, out_full, preferred_element_type=jnp.float32)
        return hidden + gate_vec * update, fresh_kv

    def head(hidden, video):
        head_in = (
            layer_norm(hidden) * (1.0 + head_rows[video, None, model_width:])
            + head_rows[video, None, :model_width]
        ).astype(jnp.bfloat16)
        velocity = jnp.dot(head_in, head_weight, preferred_element_type=jnp.float32)
        velocity = jnp.where(own_live[video][:, None], velocity, jnp.zeros_like(velocity))
        half_rows = patch_rows // 2
        returned = shifted(velocity[:half_rows].astype(jnp.bfloat16), "section", -1)
        return jnp.where(first_section, returned.astype(jnp.float32), velocity[half_rows:])

    def forward(hidden):
        return shifted(hidden.astype(jnp.bfloat16), "section", 1).astype(jnp.float32)

    hidden_a, fresh_a = layer(start_hidden[0], early, early_blocks)
    received = forward(hidden_a)
    hidden_b, fresh_b = layer(jnp.where(first_section, start_hidden[1], received), late, late_blocks)
    received = forward(hidden_b)
    first_half = head(hidden_b, 0)
    hidden_c, fresh_c = layer(received, early, early_blocks)
    second_half = head(hidden_c, 1)
    cache_buf = jnp.stack(
        [jnp.where(first_section, fresh_a, fresh_b), jnp.where(first_section, fresh_b, fresh_c)]
    )
    cache_buf = jnp.where(own_live[..., None], cache_buf, jnp.zeros_like(cache_buf))
    mine_half = jnp.stack([first_half, second_half])
    step_float = steps_idx.astype(jnp.float32)
    step_delta = sigma_of(step_float + 1.0) - sigma_of(step_float)
    new_latent = latent + step_delta[:, None, None, None] * mine_half[:, None]
    return (mine_half[:, None], new_latent, cache_buf[None, :, None])


def solution(mesh):
    in_specs = (
        P("fsdp", "patch", "section", None),
        P("fsdp", None),
        P("fsdp"),
        P(),
        P("section", "fsdp", None),
        P("section", "fsdp", None),
        P("section", None),
        P("section", None, None),
        P(),
        P(),
        P("section", "fsdp", "patch", None, None),
    )
    out_specs = (
        P("fsdp", "patch", "section", None),
        P("fsdp", "patch", "section", None),
        P("section", "fsdp", "patch", None, None),
    )
    return jax.shard_map(body, mesh=mesh, in_specs=in_specs, out_specs=out_specs, check_vma=False)
```

time: 526 us -> 299 us (0.57); the launches traced: 515 us -> 298 us
  waiting for transfers between devices: 304 us -> 170 us
  local copies, waits for them, and re-layouts: 86.2 us -> 12.4 us
  Pallas kernels: 0 us -> 28.6 us
  matrix products: 65.1 us -> 37.8 us
  other arithmetic: 30.9 us -> 18.7 us
    all_gather x3 -> x2, waiting for transfers between devices: 288 us -> 0.01 us  [the longest x1 0.01 us: body(): proj_full = lax.all_gather(wqkv[0], 'fsdp', axis=0, tiled=True)]
    ppermute x0 -> x6, waiting for transfers between devices: none -> 155 us  [around(): block = lax.ppermute(block, 'patch', ring)]
    unnamed x43 -> x47, local copies, waits for them, and re-layouts: 33 us -> 4.1 us
    pallas_call x0 -> x3, Pallas kernels: none -> 28.6 us  [attend(): pl.pallas_call(attend_kernel, grid=(steps,), in_specs=specs, out_specs=pl...]
    dot_general x13 -> x8, matrix products: 63.7 us -> 36.4 us  [the longest x3 22.3 us: layer(): projected = jnp.dot(normed, proj_full, preferred_element_type=jnp.float32)]
    slice x8 -> x7, local copies, waits for them, and re-layouts: 16.3 us -> 0.32 us  [the longest x3 0.25 us: layer(): projected[:, 2 * model_width:].astype(jnp.bfloat16)]
    dynamic_slice x3 -> x1, local copies, waits for them, and re-layouts: 16.1 us -> 0.74 us  [layer(): lax.dynamic_index_in_dim(ring_counts, video, 0, keepdims=False)]
    reduce_sum x4 -> x0, other arithmetic: 9.25 us -> none  [the longest x3 9.14 us: dense_attend(): denom_sum = jnp.sum(exp_scores, axis=-1)]
  transfers between devices with their start and end apart: 6 -> 12, of which waited for: 6 -> 10; matrix products, arithmetic and copies ran while one was open for 16% -> 14% of each run, Pallas kernels for 0% -> 3%
where the time goes in v1:
time: 299 us; the launch traced here: 298 us
  waiting for transfers between devices  170 us (57%)
  matrix products  37.8 us (13%)
  Pallas kernels  28.6 us (10%)
  other arithmetic  18.7 us (6%)
  between operations  14.5 us (5%)
  local copies, waits for them, and re-layouts  12.4 us (4%)
  starting transfers between devices  11.7 us (4%)
  blocking collectives  4.61 us (2%)
    ppermute x6, waiting for transfers between devices, around(): block = lax.ppermute(block, 'patch', ring)  155 us
    pallas_call x3, Pallas kernels, attend(): pl.pallas_call(attend_kernel, grid=(steps,), in_specs=specs, out_specs=pl...  28.6 us
    dot_general x3, matrix products, layer(): projected = jnp.dot(normed, proj_full, preferred_element_type=jnp.float32)  22.3 us
    ppermute x4, waiting for transfers between devices, shifted(): return lax.ppermute(shard, axis, pairs)  13.6 us
    dot_general x3, matrix products, layer(): update = jnp.dot(attended, out_full, preferred_element_type=jnp.float32)  13.2 us
    ppermute x4, starting transfers between devices, shifted(): return lax.ppermute(shard, axis, pairs)  8.52 us
  transfers between devices with their start and end apart: 12, of which 10 were waited for; matrix products, arithmetic and copies ran while one was open for 14% of the time, Pallas kernels for 3%

profile of v1, /device:TPU:0, one launch (start us, length us, event | category | flops | bytes accessed | tf_op | source)
XLA Modules:
  0.0 298.1 jit_solution(5452121254747690576)
XLA Ops:
  7.2 0.7 all-gather.5.cloned.1.call-update
  8.0 3.3 %dynamic-slice_bitcast_fusion = (bf16[256,3072]{1,0:T(8,128)(2,1)}, bf16[256,3072]{1,0:T(8,128)(2,1)S(1)}) fusion(bf16[1,2,1,256,3072]{4,3,2,1,0:T(8,128)(2,1)} %param.23, s32[]{:T(128)S(6)} %select_n.124, s32[]{:T(128)S(6)} %select_n.119), kind=kLoop, calls=%fused_computation.48 | loop fusion | bytes 6291464 | tf_op jit(solution)/shard_map/jit(dynamic_index_in_dim)/squeeze | solution.py:129
  11.3 3.1 %collective-permute-start = (bf16[256,3072]{1,0:T(8,128)(2,1)S(1)}, bf16[256,3072]{1,0:T(8,128)(2,1)S(1)}, u32[]{:S(2)}, u32[]{:S(2)}) collective-permute-start(bf16[256,3072]{1,0:T(8,128)(2,1)S(1)} %get-tuple-element.56), channel_id=1, source_target_pairs={{0,4},{4,8},{8,12},{12,0},{1,5},{5,9},{9,13},{13,1},{2,6},{6,10},{... | collective-permute-start | bytes 4718600 | tf_op jit(solution)/shard_map/ppermute | solution.py:134
  14.3 36.4 %collective-permute-done.refs_2_.refs_3_ = bf16[256,3072]{1,0:T(8,128)(2,1)S(1)} collective-permute-done((bf16[256,3072]{1,0:T(8,128)(2,1)S(1)}, bf16[256,3072]{1,0:T(8,128)(2,1)S(1)}, u32[]{:S(2)}, u32[]{:S(2)}) %collective-permute-start) | collective-permute-done | bytes 1572896 | tf_op jit(solution)/shard_map/ppermute | solution.py:134
  50.8 37.4 %collective-permute-done.1.refs_4_.refs_5_ = bf16[256,3072]{1,0:T(8,128)(2,1)} collective-permute-done((bf16[256,3072]{1,0:T(8,128)(2,1)S(1)}, bf16[256,3072]{1,0:T(8,128)(2,1)}, u32[]{:S(2)}, u32[]{:S(2)}) %collective-permute-start.1) | collective-permute-done | bytes 1572896 | tf_op jit(solution)/shard_map/ppermute | solution.py:134
  88.3 4.6 %all_gather.9 = bf16[2,1,256,64]{2,3,1,0:T(8,128)(2,1)S(1)} all-gather(bf16[2,1,128,64]{2,3,1,0:T(8,128)(2,1)S(1)} %convert_element_type.63), channel_id=1, replica_groups=mesh['section'=2,'patch'=4,'fsdp'=4] {'section'}, dimensions={2}, use_global_device_ids=true | all-gather | bytes 98304 | tf_op jit(solution)/shard_map/all_gather | solution.py:123
  93.7 0.7 dynamic-slice_reduce_fusion.1
  94.8 30.2 %collective-permute-done.2.refs_6_.refs_7_ = bf16[256,3072]{1,0:T(8,128)(2,1)} collective-permute-done((bf16[256,3072]{1,0:T(8,128)(2,1)}, bf16[256,3072]{1,0:T(8,128)(2,1)}, u32[]{:S(2)}, u32[]{:S(2)}) %collective-permute-start.2) | collective-permute-done | bytes 1572896 | tf_op jit(solution)/shard_map/ppermute | solution.py:134
  125.0 0.7 fusion.73
  125.9 0.6 fusion.88
  127.0 33.6 %collective-permute-done.4.refs_2_.refs_3_ = bf16[256,3072]{1,0:T(8,128)(2,1)} collective-permute-done((bf16[256,3072]{1,0:T(8,128)(2,1)S(1)}, bf16[256,3072]{1,0:T(8,128)(2,1)}, u32[]{:S(2)}, u32[]{:S(2)}) %collective-permute-start.4) | collective-permute-done | bytes 1572896 | tf_op jit(solution)/shard_map/ppermute | solution.py:134
  160.7 7.3 %fusion.4 = f32[256,4608]{1,0:T(8,128)S(1)} fusion(bf16[1,1536,4608]{2,1,0:T(8,128)(2,1)} %all-gather.5.cloned.1.call-done, f32[512,1536]{1,0:T(8,128)S(1)} %fusion.88, f32[1536]{0:T(1024)S(1)} %get-tuple-element.34, f32[1536]{0:T(1024)S(1)} %get-tuple-element.31, f32[256]{0:T(256)S(1)} %add_rsqrt_fusion.10, f32[256]{0:T(256)S(1)} %broadcast_multiply_fusion.4), kind=kOutput, calls=%fused_computation.4 | convolution fusion | flops 3625844736 | bytes 20465664 | tf_op jit(solution)/shard_map/dot_general | solution.py:164
  168.3 1.5 multiply_convert_fusion.4
  169.9 0.5 copy-done.4
  170.4 1.3 pad_maximum_fusion.refs_0_.refs_1_
  171.7 9.6 %shard_map.130 = bf16[256,1536]{1,0:T(8,128)(2,1)} custom-call(s32[4]{0:T(128)} %get-tuple-element.42.counts_ref, bf16[256,1536]{1,0:T(8,128)(2,1)} %get-tuple-element.54.q_ref, bf16[256,3072]{1,0:T(8,128)(2,1)} %pad_maximum_fusion.refs_0_.refs_1_, bf16[256,3072]{1,0:T(8,128)(2,1)} %pad_maximum_fusion.refs_0_.refs_1_, bf16[256,3072]{1,0:T(8,128)(2,1)} %copy-done.2, ...), custom_call_target="tpu_custom_call" | custom-call | flops 1610612736 | bytes 7864320 | tf_op jit(solution)/shard_map/pallas_call | solution.py:86
  181.3 4.9 %fusion.30 = bf16[256,1536]{1,0:T(8,128)(2,1)} fusion(bf16[256,1536]{1,0:T(8,128)(2,1)} %shard_map.130, bf16[1,1536,1536]{2,1,0:T(8,128)(2,1)} %all-gather.7.cloned.1.call-done, f32[512,1536]{1,0:T(8,128)S(1)} %fusion.88, f32[1536]{0:T(1024)S(1)} %get-tuple-element.32), kind=kOutput, calls=%fused_computation.19 | convolution fusion | flops 1209139200 | bytes 7870464 | tf_op jit(solution)/shard_map/dot_general | solution.py:171
  186.2 3.5 %collective-permute-start.3 = (bf16[256,1536]{1,0:T(8,128)(2,1)}, bf16[256,1536]{1,0:T(8,128)(2,1)}, u32[]{:S(2)}, u32[]{:S(2)}) collective-permute-start(bf16[256,1536]{1,0:T(8,128)(2,1)} %fusion.30), channel_id=1, source_target_pairs={{0,16},{1,17},{2,18},{3,19},{4,20},{5,21},{6,22},{7,23},{8,24},{9,... | collective-permute-start | bytes 2359304 | tf_op jit(solution)/shard_map/ppermute | solution.py:21
  189.7 5.9 %collective-permute-done.5.refs_4_.refs_5_ = bf16[256,3072]{1,0:T(8,128)(2,1)} collective-permute-done((bf16[256,3072]{1,0:T(8,128)(2,1)}, bf16[256,3072]{1,0:T(8,128)(2,1)}, u32[]{:S(2)}, u32[]{:S(2)}) %collective-permute-start.5) | collective-permute-done | bytes 1572896 | tf_op jit(solution)/shard_map/ppermute | solution.py:134
  195.6 2.4 slice_bitcast_fusion
  198.0 4.4 %collective-permute-done.3 = bf16[256,1536]{1,0:T(8,128)(2,1)} collective-permute-done((bf16[256,1536]{1,0:T(8,128)(2,1)}, bf16[256,1536]{1,0:T(8,128)(2,1)}, u32[]{:S(2)}, u32[]{:S(2)}) %collective-permute-start.3) | collective-permute-done | bytes 786464 | tf_op jit(solution)/shard_map/ppermute | solution.py:21
  202.3 1.4 fusion.85
  203.7 1.5 multiply_reduce_fusion.6
  205.3 7.6 %fusion.2 = f32[256,4608]{1,0:T(8,128)S(1)} fusion(bf16[1,1536,4608]{2,1,0:T(8,128)(2,1)} %all-gather.5.cloned.1.call-done, f32[1536]{0:T(1024)S(1)} %copy-done.19, f32[1536]{0:T(1024)S(1)} %copy-done.18, f32[256]{0:T(256)S(1)} %add_rsqrt_fusion.7, f32[256]{0:T(256)S(1)} %broadcast_multiply_fusion.3, f32[512,1536]{1,0:T(8,128)S(1)} %fusion.88, ...), kind=kOutput, calls=%fused_computation.2 | convolution fusion | flops 3626631168 | bytes 21252096 | tf_op jit(solution)/shard_map/dot_general | solution.py:164
  213.3 1.8 copy-done.3
  215.0 1.1 multiply_convert_fusion.2
  216.2 1.4 pad_maximum_fusion.1.refs_0_.refs_1_
  217.6 11.9 %collective-permute-done.6.refs_6_.refs_7_ = bf16[256,3072]{1,0:T(8,128)(2,1)S(1)} collective-permute-done((bf16[256,3072]{1,0:T(8,128)(2,1)}, bf16[256,3072]{1,0:T(8,128)(2,1)S(1)}, u32[]{:S(2)}, u32[]{:S(2)}) %collective-permute-start.6) | collective-permute-done | bytes 1572896 | tf_op jit(solution)/shard_map/ppermute | solution.py:134
  229.5 1.2 copy-done.9
  230.7 9.6 %shard_map.131 = bf16[256,1536]{1,0:T(8,128)(2,1)} custom-call(s32[4]{0:T(128)} %get-tuple-element.41.counts_ref, bf16[256,1536]{1,0:T(8,128)(2,1)} %get-tuple-element.52.q_ref, bf16[256,3072]{1,0:T(8,128)(2,1)} %pad_maximum_fusion.1.refs_0_.refs_1_, bf16[256,3072]{1,0:T(8,128)(2,1)} %pad_maximum_fusion.1.refs_0_.refs_1_, ...), custom_call_target="tpu_custom_call" | custom-call | flops 1610612736 | bytes 7864320 | tf_op jit(solution)/shard_map/pallas_call | solution.py:86
  240.2 4.3 %fusion.86 = (f32[256]{0:T(256)S(1)}, f32[256,1536]{1,0:T(8,128)S(1)}) fusion(bf16[256,1536]{1,0:T(8,128)(2,1)} %shard_map.131, bf16[1,1536,1536]{2,1,0:T(8,128)(2,1)} %all-gather.7.cloned.1.call-done, f32[1536]{0:T(1024)S(1)} %copy-done.17, bf16[256,1536]{1,0:T(8,128)(2,1)} %collective-permute-done.3, f32[512,1536]{1,0:T(8,128)S(1)} %fusion.88, pred[]{:T(512)S(6)} %eq.21), kind=kOutput, calls=%fused_computation.155 | convolution fusion | flops 1209925376 | bytes 9444353 | tf_op jit(solution)/shard_map/dot_general | solution.py:171
  244.9 2.2 collective-permute-start.8
  247.5 1.5 collective-permute-start.7
  249.1 1.5 slice_bitcast_fusion.1
  250.6 2.6 collective-permute-done.7
  253.2 5.2 %collective-permute-done.8 = bf16[256,1536]{1,0:T(8,128)(2,1)S(1)} collective-permute-done((bf16[256,1536]{1,0:T(8,128)(2,1)S(1)}, bf16[256,1536]{1,0:T(8,128)(2,1)S(1)}, u32[]{:S(2)}, u32[]{:S(2)}) %collective-permute-start.8) | collective-permute-done | bytes 786464 | tf_op jit(solution)/shard_map/ppermute | solution.py:21
  258.9 7.4 %fusion = f32[256,4608]{1,0:T(8,128)S(1)} fusion(bf16[1,1536,4608]{2,1,0:T(8,128)(2,1)} %all-gather.5.cloned.1.call-done, bf16[256,1536]{1,0:T(8,128)(2,1)S(1)} %collective-permute-done.8, f32[256]{0:T(256)S(1)} %add_rsqrt_fusion.3, f32[256]{0:T(256)S(1)} %broadcast_multiply_fusion.1, f32[1536]{0:T(1024)S(1)} %get-tuple-element.34, f32[1536]{0:T(1024)S(1)} %get-tuple-element.31), kind=kOutput, calls=%fused_computation | convolution fusion | flops 3626237952 | bytes 19675136 | tf_op jit(solution)/shard_map/dot_general | solution.py:164
  266.8 1.1 multiply_convert_fusion
  267.9 1.4 pad_maximum_fusion.2.refs_0_.refs_1_
  269.3 9.5 %shard_map.132 = bf16[256,1536]{1,0:T(8,128)(2,1)} custom-call(s32[4]{0:T(128)} %get-tuple-element.42.counts_ref, bf16[256,1536]{1,0:T(8,128)(2,1)} %get-tuple-element.50.q_ref, bf16[256,3072]{1,0:T(8,128)(2,1)} %pad_maximum_fusion.2.refs_0_.refs_1_, bf16[256,3072]{1,0:T(8,128)(2,1)} %pad_maximum_fusion.2.refs_0_.refs_1_, bf16[256,3072]{1,0:T(8,128)(2,1)} %copy-done.2, ...), custom_call_target="tpu_custom_call" | custom-call | flops 1610612736 | bytes 7864320 | tf_op jit(solution)/shard_map/pallas_call | solution.py:86
  278.8 4.1 %fusion.87 = (f32[256]{0:T(256)S(1)}, f32[256,1536]{1,0:T(8,128)S(1)}) fusion(bf16[256,1536]{1,0:T(8,128)(2,1)} %shard_map.132, bf16[1,1536,1536]{2,1,0:T(8,128)(2,1)} %all-gather.7.cloned.1.call-done, f32[1536]{0:T(1024)S(1)} %get-tuple-element.32, bf16[256,1536]{1,0:T(8,128)(2,1)S(1)} %collective-permute-done.8), kind=kOutput, calls=%fused_computation.156 | convolution fusion | flops 1209532160 | bytes 7871488 | tf_op jit(solution)/shard_map/dot_general | solution.py:171
  283.2 0.6 copy-done.22
  284.3 1.3 collective-permute-start.9
  285.6 0.9 fusion.39
  286.5 2.1 maximum_select_fusion
  288.6 1.3 collective-permute-done.9
  289.9 0.6 maximum_bitcast_fusion
  290.6 0.7 fusion.63
  (98 shorter events, 5.4 us)
Async XLA Ops:
  7.2 87.3 %copy-start = (f32[50,3072]{1,0:T(8,128)S(1)}, f32[50,3072]{1,0:T(8,128)}, u32[]{:S(2)}) copy-start(f32[50,3072]{1,0:T(8,128)} %param.21) | copy-start | bytes 1843204
  7.2 153.5 %all-gather.5.cloned.1.call-start = ((), (), s32[]{:S(2)}) async-start(), calls=%async_computation | async-start | bytes 17694720 | tf_op jit(solution)/shard_map/all_gather | solution.py:124
  7.9 173.4 %all-gather.7.cloned.1.call-start = ((), (), s32[]{:S(2)}) async-start(), calls=%async_computation.1 | async-start | bytes 5898240 | tf_op jit(solution)/shard_map/all_gather | solution.py:125
  8.0 80.3 %copy-start.13 = (f32[2,1,128,64]{2,3,1,0:T(8,128)S(1)}, f32[2,1,128,64]{2,3,1,0:T(8,128)}, u32[]{:S(2)}) copy-start(f32[2,1,128,64]{2,3,1,0:T(8,128)} %param.13) | copy-start | bytes 196612
  11.2 81.7 %copy-start.15 = (s32[2,4]{1,0:T(2,128)S(1)}, s32[2,4]{1,0:T(2,128)}, u32[]{:S(2)}) copy-start(s32[2,4]{1,0:T(2,128)} %param.14) | copy-start | bytes 100
  11.2 82.0 %copy-start.12 = (f32[1,50,4608]{2,0,1:T(1,128)S(1)}, f32[1,50,4608]{2,0,1:T(1,128)}, u32[]{:S(2)}) copy-start(f32[1,50,4608]{2,0,1:T(1,128)} %param.20) | copy-start | bytes 2764804
  11.2 82.0 %copy-start.20 = (s32[2]{0:T(128)S(1)}, s32[2]{0:T(128)}, u32[]{:S(2)}) copy-start(s32[2]{0:T(128)} %param.15) | copy-start | bytes 28
  11.2 114.5 %copy-start.16 = (f32[1,3072]{1,0:T(1,128)S(1)}, f32[1,3072]{1,0:T(1,128)}, u32[]{:S(2)}) copy-start(f32[1,3072]{1,0:T(1,128)} %param.19) | copy-start | bytes 36868
  11.3 39.5 %collective-permute-start = (bf16[256,3072]{1,0:T(8,128)(2,1)S(1)}, bf16[256,3072]{1,0:T(8,128)(2,1)S(1)}, u32[]{:S(2)}, u32[]{:S(2)}) collective-permute-start(bf16[256,3072]{1,0:T(8,128)(2,1)S(1)} %get-tuple-element.56), channel_id=1, source_target_pairs={{0,4},{4,8},{8,12},{12,0},{1,5},{5,9},{9,13},{13,1},{2,6},{6,10},{... | collective-permute-start | bytes 4718600 | tf_op jit(solution)/shard_map/ppermute | solution.py:134
  50.8 44.0 %copy-start.2 = (bf16[256,3072]{1,0:T(8,128)(2,1)}, bf16[256,3072]{1,0:T(8,128)(2,1)S(1)}, u32[]{:S(2)}) copy-start(bf16[256,3072]{1,0:T(8,128)(2,1)S(1)} %collective-permute-done.refs_2_.refs_3_) | copy-start | bytes 4718596
  50.8 37.5 %collective-permute-start.1 = (bf16[256,3072]{1,0:T(8,128)(2,1)S(1)}, bf16[256,3072]{1,0:T(8,128)(2,1)}, u32[]{:S(2)}, u32[]{:S(2)}) collective-permute-start(bf16[256,3072]{1,0:T(8,128)(2,1)S(1)} %collective-permute-done.refs_2_.refs_3_), channel_id=1, source_target_pairs={{0,4},{4,8},{8,12},{12,0},{1,5},{5,9},{9,13},{13,1},{2,6},{6,10},{... | collective-permute-start | bytes 4718600 | tf_op jit(solution)/shard_map/ppermute | solution.py:134
  50.8 75.1 %copy-start.14 = (bf16[64,1536]{1,0:T(8,128)(2,1)S(1)}, bf16[64,1536]{1,0:T(8,128)(2,1)}, u32[]{:S(2)}) copy-start(bf16[64,1536]{1,0:T(8,128)(2,1)} %param.16) | copy-start | bytes 589828
  88.2 36.8 %collective-permute-start.2 = (bf16[256,3072]{1,0:T(8,128)(2,1)}, bf16[256,3072]{1,0:T(8,128)(2,1)}, u32[]{:S(2)}, u32[]{:S(2)}) collective-permute-start(bf16[256,3072]{1,0:T(8,128)(2,1)} %collective-permute-done.1.refs_4_.refs_5_), channel_id=1, source_target_pairs={{0,4},{4,8},{8,12},{12,0},{1,5},{5,9},{9,13},{13,1},{2,6},{6,10},{... | collective-permute-start | bytes 4718600 | tf_op jit(solution)/shard_map/ppermute | solution.py:134
  93.0 32.0 %copy-start.11 = (bf16[256,3072]{1,0:T(8,128)(2,1)S(1)}, bf16[256,3072]{1,0:T(8,128)(2,1)}, u32[]{:S(2)}) copy-start(bf16[256,3072]{1,0:T(8,128)(2,1)} %get-tuple-element.5) | copy-start | bytes 4718596
  125.0 35.6 %collective-permute-start.4 = (bf16[256,3072]{1,0:T(8,128)(2,1)S(1)}, bf16[256,3072]{1,0:T(8,128)(2,1)}, u32[]{:S(2)}, u32[]{:S(2)}) collective-permute-start(bf16[256,3072]{1,0:T(8,128)(2,1)S(1)} %copy-done.11), channel_id=1, source_target_pairs={{0,4},{4,8},{8,12},{12,0},{1,5},{5,9},{9,13},{13,1},{2,6},{6,10},{... | collective-permute-start | bytes 4718600 | tf_op jit(solution)/shard_map/ppermute | solution.py:134
  160.7 34.9 %collective-permute-start.5 = (bf16[256,3072]{1,0:T(8,128)(2,1)}, bf16[256,3072]{1,0:T(8,128)(2,1)}, u32[]{:S(2)}, u32[]{:S(2)}) collective-permute-start(bf16[256,3072]{1,0:T(8,128)(2,1)} %collective-permute-done.4.refs_2_.refs_3_), channel_id=1, source_target_pairs={{0,4},{4,8},{8,12},{12,0},{1,5},{5,9},{9,13},{13,1},{2,6},{6,10},{... | collective-permute-start | bytes 4718600 | tf_op jit(solution)/shard_map/ppermute | solution.py:134
  168.0 2.4 copy-start.4
  169.8 1.9 copy-start.5
  186.2 16.2 %collective-permute-start.3 = (bf16[256,1536]{1,0:T(8,128)(2,1)}, bf16[256,1536]{1,0:T(8,128)(2,1)}, u32[]{:S(2)}, u32[]{:S(2)}) collective-permute-start(bf16[256,1536]{1,0:T(8,128)(2,1)} %fusion.30), channel_id=1, source_target_pairs={{0,16},{1,17},{2,18},{3,19},{4,20},{5,21},{6,22},{7,23},{8,24},{9,... | collective-permute-start | bytes 2359304 | tf_op jit(solution)/shard_map/ppermute | solution.py:21
  195.6 33.9 %collective-permute-start.6 = (bf16[256,3072]{1,0:T(8,128)(2,1)}, bf16[256,3072]{1,0:T(8,128)(2,1)S(1)}, u32[]{:S(2)}, u32[]{:S(2)}) collective-permute-start(bf16[256,3072]{1,0:T(8,128)(2,1)} %collective-permute-done.5.refs_4_.refs_5_), channel_id=1, source_target_pairs={{0,4},{4,8},{8,12},{12,0},{1,5},{5,9},{9,13},{13,1},{2,6},{6,10},{... | collective-permute-start | bytes 4718600 | tf_op jit(solution)/shard_map/ppermute | solution.py:134
  203.7 1.5 copy-start.18
  203.7 1.5 copy-start.19
  212.9 2.2 copy-start.3
  216.2 1.4 copy-start.7
  229.5 1.2 copy-start.9
  230.7 9.6 %copy-start.17 = (f32[1536]{0:T(1024)S(1)}, f32[1536]{0:T(1024)}, u32[]{:S(2)}) copy-start(f32[1536]{0:T(1024)} %get-tuple-element.29) | copy-start | bytes 18436
  244.5 2.5 copy-start.21
  244.9 13.5 %collective-permute-start.8 = (bf16[256,1536]{1,0:T(8,128)(2,1)S(1)}, bf16[256,1536]{1,0:T(8,128)(2,1)S(1)}, u32[]{:S(2)}, u32[]{:S(2)}) collective-permute-start(bf16[256,1536]{1,0:T(8,128)(2,1)S(1)} %get-tuple-element.60), channel_id=1, source_target_pairs={{0,16},{1,17},{2,18},{3,19},{4,20},{5,21},{6,22},{7,23},{8,24},{9,... | collective-permute-start | bytes 2359304 | tf_op jit(solution)/shard_map/ppermute | solution.py:21
  247.5 5.6 %collective-permute-start.7 = (bf16[128,64]{0,1:T(8,128)(2,1)S(1)}, bf16[128,64]{0,1:T(8,128)(2,1)S(1)}, u32[]{:S(2)}, u32[]{:S(2)}) collective-permute-start(bf16[128,64]{0,1:T(8,128)(2,1)S(1)} %slice.218), channel_id=1, source_target_pairs={{16,0},{17,1},{18,2},{19,3},{20,4},{21,5},{22,6},{23,7},{24,8},{25... | collective-permute-start | bytes 49160 | tf_op jit(solution)/shard_map/ppermute | solution.py:21
  282.8 0.9 copy-start.22
  282.9 2.7 copy-start.6
  282.9 2.7 copy-start.8
  282.9 2.7 copy-start.10
  284.3 5.6 %collective-permute-start.9 = (bf16[128,64]{0,1:T(8,128)(2,1)S(1)}, bf16[128,64]{0,1:T(8,128)(2,1)S(1)}, u32[]{:S(2)}, u32[]{:S(2)}) collective-permute-start(bf16[128,64]{0,1:T(8,128)(2,1)S(1)} %slice.217), channel_id=1, source_target_pairs={{16,0},{17,1},{18,2},{19,3},{20,4},{21,5},{22,6},{23,7},{24,8},{25... | collective-permute-start | bytes 49160 | tf_op jit(solution)/shard_map/ppermute | solution.py:21
  286.5 4.8 %copy-start.1 = (f32[50,3072]{1,0:T(8,128)S(1)}, f32[50,3072]{1,0:T(8,128)}, u32[]{:S(2)}) copy-start(f32[50,3072]{1,0:T(8,128)} %param.21) | copy-start | bytes 1843204
Sparse Core Ops, SparseCore 0:
  9.6 93.7 all-gather.4
  104.9 37.4 all-gather.6

commit v2 on v1

--- a/solution.py
+++ b/solution.py
@@ -40,11 +40,14 @@
 
 
 HEADS_STEP = 2
+WIDE = 8
 
 
 def attend_kernel(counts_ref, q_ref, *refs):
     blocks = (len(refs) - 1) // 2
     out_ref = refs[-1]
+    slot = lax.broadcasted_iota(jnp.int32, (1, refs[0].shape[0]), 1)
+    bias = [jnp.where(slot < counts_ref[b], 0.0, -jnp.inf) for b in range(blocks)]
     for head in range(q_ref.shape[1] // HD):
         cols = slice(head * HD, (head + 1) * HD)
         query = q_ref[:, cols]
@@ -52,9 +55,8 @@
         for b in range(blocks):
             score = lax.dot_general(
                 query, refs[2 * b][:, cols], (((1,), (1,)), ((), ())), preferred_element_type=jnp.float32
-            ) * (1.0 / math.sqrt(HD))
-            slot = lax.broadcasted_iota(jnp.int32, score.shape, 1)
-            scores.append(jnp.where(slot < counts_ref[b], score, -jnp.inf))
+            )
+            scores.append(score * (math.log2(math.e) / math.sqrt(HD)) + bias[b])
         top = scores[0]
         for score in scores[1:]:
             top = jnp.maximum(top, score)
@@ -62,7 +64,7 @@
         total = None
         mixed = None
         for b in range(blocks):
-            weight = jnp.exp(scores[b] - top)
+            weight = jnp.exp2(scores[b] - top)
             part = jnp.dot(
                 weight.astype(jnp.bfloat16), refs[2 * b + 1][:, cols], preferred_element_type=jnp.float32
             )
@@ -72,27 +74,32 @@
         out_ref[:, cols] = (mixed / denom).astype(jnp.bfloat16)
 
 
-def attend(queries, kv_blocks, block_counts):
-    rows, model_width = queries.shape
+def attend(heads, queries, q_head, kv_blocks, block_counts):
+    rows = queries.shape[0]
     cols = HEADS_STEP * HD
-    steps = model_width // cols
-    specs = [pl.BlockSpec(memory_space=pltpu.SMEM), pl.BlockSpec((rows, cols), lambda h: (0, h))]
+    steps = heads // HEADS_STEP
+
+    def spec(array, first_head):
+        first = first_head // HEADS_STEP
+        return pl.BlockSpec((array.shape[0], cols), lambda h: (0, h + first))
+
+    specs = [pl.BlockSpec(memory_space=pltpu.SMEM), spec(queries, q_head)]
     operands = [block_counts, queries]
-    for kv in kv_blocks:
-        specs.append(pl.BlockSpec((kv.shape[0], cols), lambda h: (0, h)))
-        specs.append(pl.BlockSpec((kv.shape[0], cols), lambda h: (0, h + steps)))
+    for kv, key_head, value_head in kv_blocks:
+        specs += [spec(kv, key_head), spec(kv, value_head)]
         operands += [kv, kv]
-    keys = sum(kv.shape[0] for kv in kv_blocks)
+    keys = sum(kv.shape[0] for kv, _, _ in kv_blocks)
+    width = heads * HD
     return pl.pallas_call(
         attend_kernel,
         grid=(steps,),
         in_specs=specs,
         out_specs=pl.BlockSpec((rows, cols), lambda h: (0, h)),
-        out_shape=jax.ShapeDtypeStruct((rows, model_width), jnp.bfloat16),
+        out_shape=jax.ShapeDtypeStruct((rows, width), jnp.bfloat16),
         cost_estimate=pl.CostEstimate(
-            flops=4 * rows * keys * model_width,
-            bytes_accessed=4 * (rows + keys) * model_width,
-            transcendentals=rows * keys * HEADS,
+            flops=4 * rows * keys * width,
+            bytes_accessed=4 * (rows + keys) * width,
+            transcendentals=rows * keys * heads,
         ),
     )(*operands)
 
@@ -114,7 +121,7 @@
     own_patch = lax.axis_index("patch")
     first_section = section_index == 0
     videos = latent.shape[0]
-    assert videos == 2 and lax.axis_size("section") == 2
+    assert videos == 2 and lax.axis_size("section") == 2 and counts.shape[1] == 4
     patch_rows = stale_cache.shape[3]
     model_width = embed_weight.shape[1]
     patch_count = counts.shape[1]
@@ -124,19 +131,11 @@
     proj_full = lax.all_gather(wqkv[0], "fsdp", axis=0, tiled=True)
     out_full = lax.all_gather(wo[0], "fsdp", axis=0, tiled=True)
     ring = [(i, (i + 1) % patch_count) for i in range(patch_count)]
-
-    def around(video, after=None):
-        block = lax.dynamic_index_in_dim(stale_cache[0, :, 0], video, 0, keepdims=False)
-        if after is not None:
-            block, _ = lax.optimization_barrier((block, after))
-        blocks = []
-        for _ in range(patch_count - 1):
-            block = lax.ppermute(block, "patch", ring)
-            blocks.append(block)
-        return blocks
-
-    early_blocks = around(early)
-    late_blocks = around(late, early_blocks[-1])
+    early_blocks = []
+    block = lax.dynamic_index_in_dim(stale_cache[0, :, 0], early, 0, keepdims=False)
+    for _ in range(patch_count - 1):
+        block = lax.ppermute(block, "patch", ring)
+        early_blocks.append(block)
 
     start_hidden = jnp.dot(
         rows_full.reshape(-1, rows_full.shape[3]), embed_weight, preferred_element_type=jnp.float32
@@ -154,12 +153,13 @@
     )
     own_live = slot_iota[None, :] < ring_counts[:, :1]
 
-    def layer(hidden, video, stale_blocks):
+    def counts_of(video):
+        return lax.dynamic_index_in_dim(ring_counts, video, 0, keepdims=False)
+
+    def project(hidden, video):
         mod = lax.dynamic_index_in_dim(modulation_all, video, 0)
-        block_counts = lax.dynamic_index_in_dim(ring_counts, video, 0, keepdims=False)
         shift_vec = mod[:, :model_width]
         scale_vec = mod[:, model_width : 2 * model_width]
-        gate_vec = mod[:, 2 * model_width :]
         normed = (layer_norm(hidden) * (1.0 + scale_vec) + shift_vec).astype(jnp.bfloat16)
         projected = jnp.dot(normed, proj_full, preferred_element_type=jnp.float32)
         queries = rms_norm(projected[:, :model_width], gain_rows[:model_width]).astype(jnp.bfloat16)
@@ -167,9 +167,15 @@
         fresh_kv = jnp.concatenate(
             [keys.astype(jnp.bfloat16), projected[:, 2 * model_width :].astype(jnp.bfloat16)], axis=-1
         )
-        attended = attend(queries, [fresh_kv] + stale_blocks, block_counts)
-        update = jnp.dot(attended, out_full, preferred_element_type=jnp.float32)
-        return hidden + gate_vec * update, fresh_kv
+        return queries, fresh_kv
+
+    def finish(hidden, attended, video):
+        gate_vec = lax.dynamic_index_in_dim(modulation_all, video, 0)[:, 2 * model_width :]
+        return hidden + gate_vec * jnp.dot(attended, out_full, preferred_element_type=jnp.float32)
+
+    def attend_early(queries, fresh_kv):
+        blocks = [(kv, 0, HEADS) for kv in [fresh_kv] + early_blocks]
+        return attend(HEADS, queries, 0, blocks, counts_of(early))
 
     def head(hidden, video):
         head_in = (
@@ -185,12 +191,107 @@
     def forward(hidden):
         return shifted(hidden.astype(jnp.bfloat16), "section", 1).astype(jnp.float32)
 
-    hidden_a, fresh_a = layer(start_hidden[0], early, early_blocks)
+    def after(value, *earlier):
+        return lax.optimization_barrier((value,) + earlier)[0]
+
+    def send(value, pairs):
+        return lax.ppermute(value, "patch", pairs)
+
+    def pick(array, first_head, heads):
+        first = first_head * HD
+        return jnp.concatenate(
+            [array[:, first : first + heads * HD], array[:, model_width + first : model_width + first + heads * HD]],
+            axis=-1,
+        )
+
+    queries_a, fresh_a = project(start_hidden[0], early)
+    late_stale = lax.dynamic_index_in_dim(stale_cache[0, :, 0], late, 0, keepdims=False)
+    narrow = HEADS - WIDE
+    halves = [pick(late_stale, first, WIDE // 2) for first in (0, WIDE // 2)]
+    narrow_own = pick(late_stale, WIDE, narrow)
+    queries_a, *halves = lax.optimization_barrier((queries_a, *halves))
+    halves = [after(half, early_blocks[-1]) for half in halves]
+    right_1 = [send(half, [(0, 1), (1, 2), (2, 3)]) for half in halves]
+    left_1 = [send(half, [(3, 2), (2, 1), (1, 0)]) for half in halves]
+    attended_a = attend_early(queries_a, fresh_a)
+    attended_a, right_1[0], left_1[0] = lax.optimization_barrier((attended_a, right_1[0], left_1[0]))
+    right_2 = [send(right_1[0], [(1, 2), (2, 3)]), None]
+    left_2 = [send(left_1[0], [(2, 1), (1, 0)]), None]
+    hidden_a = finish(start_hidden[0], attended_a, early)
     received = forward(hidden_a)
-    hidden_b, fresh_b = layer(jnp.where(first_section, start_hidden[1], received), late, late_blocks)
+    hidden_b = jnp.where(first_section, start_hidden[1], received)
+    hidden_b, right_1[1], left_1[1] = lax.optimization_barrier((hidden_b, right_1[1], left_1[1]))
+    right_2[1] = send(right_1[1], [(1, 2), (2, 3)])
+    left_2[1] = send(left_1[1], [(2, 1), (1, 0)])
+    queries_b, fresh_b = project(hidden_b, late)
+    queries_b, right_2[0], left_2[0] = lax.optimization_barrier((queries_b, right_2[0], left_2[0]))
+    right_3 = [send(right_2[0], [(2, 3)]), None]
+    left_3 = [send(left_2[0], [(1, 0)]), None]
+    packed = jnp.concatenate([queries_b[:, WIDE * HD :], pick(fresh_b, WIDE, narrow)], axis=-1)
+    guest = send(packed, [(0, 1), (3, 2)])
+    right_3[1] = send(after(right_2[1], packed), [(2, 3)])
+    left_3[1] = send(after(left_2[1], packed), [(1, 0)])
+    narrow_own = after(narrow_own, right_2[0], left_2[0], queries_b)
+    narrow_r1 = send(narrow_own, [(0, 1), (1, 2)])
+    narrow_l1 = send(narrow_own, [(3, 2), (2, 1)])
+    packed = jnp.concatenate([queries_b[:, WIDE * HD :], pick(fresh_b, WIDE, narrow)], axis=-1)
+    guest = send(packed, [(0, 1), (3, 2)])
+    narrow_r2 = send(narrow_r1, [(1, 2)])
+    narrow_l2 = send(narrow_l1, [(2, 1)])
+    narrow_2 = jnp.where(own_patch >= 2, narrow_r2, narrow_l2)
+    guest_far = jnp.where(own_patch == 1, narrow_l1, narrow_r1)
+    late_counts = counts_of(late)
+    guest_patch = jnp.where(own_patch == 1, 1, 3)
+    guest_counts = jnp.stack(
+        [late_counts[guest_patch], late_counts[0], late_counts[2], late_counts[4 - guest_patch]]
+    )
+    guest_out = attend(
+        narrow,
+        guest,
+        0,
+        [
+            (guest, narrow, 2 * narrow),
+            (late_stale, WIDE, HEADS + WIDE),
+            (narrow_2, 0, narrow),
+            (guest_far, 0, narrow),
+        ],
+        guest_counts,
+    )
+    returned = send(guest_out, [(1, 0), (2, 3)])
+    narrow_out = attend(
+        narrow,
+        queries_b,
+        WIDE,
+        [
+            (fresh_b, WIDE, HEADS + WIDE),
+            (narrow_r1, 0, narrow),
+            (narrow_2, 0, narrow),
+            (narrow_l1, 0, narrow),
+        ],
+        late_counts,
+    )
+    wide_out = [
+        attend(
+            WIDE // 2,
+            queries_b,
+            h * (WIDE // 2),
+            [
+                (fresh_b, h * (WIDE // 2), HEADS + h * (WIDE // 2)),
+                (jnp.where(own_patch >= 1, right_1[h], left_3[h]), 0, WIDE // 2),
+                (jnp.where(own_patch >= 2, right_2[h], left_2[h]), 0, WIDE // 2),
+                (jnp.where(own_patch >= 3, right_3[h], left_1[h]), 0, WIDE // 2),
+            ],
+            late_counts,
+        )
+        for h in (0, 1)
+    ]
+    is_middle = (own_patch == 1) | (own_patch == 2)
+    attended_b = jnp.concatenate([*wide_out, jnp.where(is_middle, narrow_out, returned)], axis=-1)
+    hidden_b = finish(hidden_b, attended_b, late)
     received = forward(hidden_b)
     first_half = head(hidden_b, 0)
-    hidden_c, fresh_c = layer(received, early, early_blocks)
+    queries_c, fresh_c = project(received, early)
+    hidden_c = finish(received, attend_early(queries_c, fresh_c), early)
     second_half = head(hidden_c, 1)
     cache_buf = jnp.stack(
         [jnp.where(first_section, fresh_a, fresh_b), jnp.where(first_section, fresh_b, fresh_c)]

time: 299 us -> 312 us (1.043)
  the two profiles are of different devices: /device:TPU:0 before, /device:TPU:8 now
where the time goes in v2:
time: 312 us; the launch traced here: 311 us
  waiting for transfers between devices  106 us (34%)
  starting transfers between devices  64.5 us (21%)
  matrix products  37.3 us (12%)
  Pallas kernels  36.4 us (12%)
  other arithmetic  34.2 us (11%)
  between operations  14.8 us (5%)
  local copies, waits for them, and re-layouts  13.3 us (4%)
  blocking collectives  4.61 us (1%)
    ppermute x3, waiting for transfers between devices, body(): block = lax.ppermute(block, 'patch', ring)  67.3 us
    ppermute x18, starting transfers between devices, send(): return lax.ppermute(value, 'patch', pairs)  52.2 us
    pallas_call x6, Pallas kernels, attend(): pl.pallas_call(attend_kernel, grid=(steps,), in_specs=specs, out_specs=pl...  36.4 us
    dot_general x3, matrix products, project(): projected = jnp.dot(normed, proj_full, preferred_element_type=jnp.float32)  22.4 us
    all_gather x1, waiting for transfers between devices, body(): proj_full = lax.all_gather(wqkv[0], 'fsdp', axis=0, tiled=True)  16.2 us
    dot_general x3, matrix products, finish(): jnp.dot(attended, out_full, preferred_element_type=jnp.float32)  12.5 us
    ppermute x4, waiting for transfers between devices, shifted(): return lax.ppermute(shard, axis, pairs)  10.5 us
    ppermute x18, waiting for transfers between devices, send(): return lax.ppermute(value, 'patch', pairs)  10 us
  transfers between devices with their start and end apart: 27, of which 12 were waited for; matrix products, arithmetic and copies ran while one was open for 17% of the time, Pallas kernels for 9%

profile of v2, /device:TPU:8, one launch (start us, length us, event | category | flops | bytes accessed | tf_op | source)
XLA Modules:
  0.0 310.8 jit_solution(12012359795130597115)
XLA Ops:
  8.7 3.3 %dynamic-slice_bitcast_fusion = (bf16[256,3072]{1,0:T(8,128)(2,1)}, bf16[256,3072]{1,0:T(8,128)(2,1)S(1)}) fusion(bf16[1,2,1,256,3072]{4,3,2,1,0:T(8,128)(2,1)} %param.23, s32[]{:T(128)S(6)} %select_n.186, s32[]{:T(128)S(6)} %select_n.190), kind=kLoop, calls=%fused_computation.53 | loop fusion | bytes 6291464 | tf_op jit(solution)/shard_map/jit(dynamic_index_in_dim)/squeeze | solution.py:135
  12.0 1.6 collective-permute-start
  15.2 33.3 %collective-permute-done.refs_2_.refs_3_ = bf16[256,3072]{1,0:T(8,128)(2,1)} collective-permute-done((bf16[256,3072]{1,0:T(8,128)(2,1)}, bf16[256,3072]{1,0:T(8,128)(2,1)}, u32[]{:S(2)}, u32[]{:S(2)}) %collective-permute-start) | collective-permute-done | bytes 1572896 | tf_op jit(solution)/shard_map/ppermute | solution.py:137
  48.5 1.6 collective-permute-start.1
  50.7 4.6 %all_gather.9 = bf16[2,1,256,64]{2,3,1,0:T(8,128)(2,1)S(1)} all-gather(bf16[2,1,128,64]{2,3,1,0:T(8,128)(2,1)S(1)} %convert_element_type.63), channel_id=1, replica_groups=mesh['section'=2,'patch'=4,'fsdp'=4] {'section'}, dimensions={2}, use_global_device_ids=true | all-gather | bytes 98304 | tf_op jit(solution)/shard_map/all_gather | solution.py:130
  59.7 25.3 %collective-permute-done.1.refs_4_.refs_5_ = bf16[256,3072]{1,0:T(8,128)(2,1)} collective-permute-done((bf16[256,3072]{1,0:T(8,128)(2,1)}, bf16[256,3072]{1,0:T(8,128)(2,1)}, u32[]{:S(2)}, u32[]{:S(2)}) %collective-permute-start.1) | collective-permute-done | bytes 1572896 | tf_op jit(solution)/shard_map/ppermute | solution.py:137
  85.6 16.2 %all-gather.5.cloned.1.call-done = bf16[1,1536,4608]{2,1,0:T(8,128)(2,1)} async-done(((bf16[1,384,4608]{2,1,0:T(8,128)(2,1)}), bf16[1,1536,4608]{2,1,0:T(8,128)(2,1)}) %all-gather.5.cloned.1.call-update) | async-done | bytes 14155792 | tf_op jit(solution)/shard_map/all_gather | solution.py:131
  101.8 7.8 %fusion.4 = f32[256,4608]{1,0:T(8,128)S(1)} fusion(bf16[1,1536,4608]{2,1,0:T(8,128)(2,1)} %all-gather.5.cloned.1.call-done, f32[512,1536]{1,0:T(8,128)} %copy-done.4, f32[1536]{0:T(1024)S(1)} %get-tuple-element.66, f32[1536]{0:T(1024)S(1)} %get-tuple-element.63, f32[256]{0:T(256)S(1)} %add_rsqrt_fusion.10, f32[256]{0:T(256)S(1)} %broadcast_multiply_fusion.4), kind=kOutput, calls=%fused_computation.4 | convolution fusion | flops 3625844736 | bytes 20461568 | tf_op jit(solution)/shard_map/dot_general | solution.py:164
  110.0 1.8 copy-done.7
  112.9 8.7 %collective-permute-done.2.refs_6_.refs_7_ = bf16[256,3072]{1,0:T(8,128)(2,1)S(1)} collective-permute-done((bf16[256,3072]{1,0:T(8,128)(2,1)}, bf16[256,3072]{1,0:T(8,128)(2,1)S(1)}, u32[]{:S(2)}, u32[]{:S(2)}) %collective-permute-start.2) | collective-permute-done | bytes 1572896 | tf_op jit(solution)/shard_map/ppermute | solution.py:137
  121.6 6.0 %collective-permute-start.4 = (bf16[256,1024]{1,0:T(8,128)(2,1)}, bf16[256,1024]{1,0:T(8,128)(2,1)S(1)}, u32[]{:S(2)}, u32[]{:S(2)}) collective-permute-start(bf16[256,1024]{1,0:T(8,128)(2,1)} %get-tuple-element.23), channel_id=1, source_target_pairs={{12,8},{8,4},{4,0},{13,9},{9,5},{5,1},{14,10},{10,6},{6,2},{15,11}... | collective-permute-start | bytes 1572872 | tf_op jit(solution)/shard_map/ppermute | solution.py:198
  127.6 1.9 collective-permute-start.3
  130.9 9.4 %shard_map.130 = bf16[256,1536]{1,0:T(8,128)(2,1)} custom-call(s32[4]{0:T(128)} %get-tuple-element.109.counts_ref, bf16[256,1536]{1,0:T(8,128)(2,1)} %get-tuple-element.21.q_ref, bf16[256,3072]{1,0:T(8,128)(2,1)} %pad_maximum_fusion.refs_0_.refs_1_, bf16[256,3072]{1,0:T(8,128)(2,1)} %pad_maximum_fusion.refs_0_.refs_1_, ...), custom_call_target="tpu_custom_call" | custom-call | flops 1610612736 | bytes 7864320 | tf_op jit(solution)/shard_map/pallas_call | solution.py:93
  140.9 4.6 %fusion.30 = bf16[256,1536]{1,0:T(8,128)(2,1)S(1)} fusion(bf16[256,1536]{1,0:T(8,128)(2,1)} %shard_map.130, bf16[1,1536,1536]{2,1,0:T(8,128)(2,1)} %all-gather.7.cloned.1.call-done, f32[512,1536]{1,0:T(8,128)} %copy-done.4, f32[1536]{0:T(1024)S(1)} %get-tuple-element.64), kind=kOutput, calls=%fused_computation.19 | convolution fusion | flops 1209139200 | bytes 7870464 | tf_op jit(solution)/shard_map/dot_general | solution.py:174
  145.5 3.6 %collective-permute-start.5 = (bf16[256,1536]{1,0:T(8,128)(2,1)S(1)}, bf16[256,1536]{1,0:T(8,128)(2,1)S(1)}, u32[]{:S(2)}, u32[]{:S(2)}) collective-permute-start(bf16[256,1536]{1,0:T(8,128)(2,1)S(1)} %fusion.30), channel_id=1, source_target_pairs={{0,16},{1,17},{2,18},{3,19},{4,20},{5,21},{6,22},{7,23},{8,24},{9,... | collective-permute-start | bytes 2359304 | tf_op jit(solution)/shard_map/ppermute | solution.py:21
  149.0 3.3 %pad_add_fusion.1.counts_ref = s32[4]{0:T(128)} fusion(s32[1]{0:T(128)} %bitcast.7, s32[1]{0:T(128)} %bitcast.6, s32[1]{0:T(128)} %bitcast.5, s32[1]{0:T(128)} %bitcast.4), kind=kLoop, calls=%fused_computation.162 | loop fusion | flops 12 | bytes 32 | tf_op jit(solution)/shard_map/stack | solution.py:245
  153.6 4.0 %collective-permute-start.7 = (bf16[256,1024]{1,0:T(8,128)(2,1)S(1)}, bf16[256,1024]{1,0:T(8,128)(2,1)S(1)}, u32[]{:S(2)}, u32[]{:S(2)}) collective-permute-start(bf16[256,1024]{1,0:T(8,128)(2,1)S(1)} %copy-done.21), channel_id=1, source_target_pairs={{12,8},{8,4},{4,0},{13,9},{9,5},{5,1},{14,10},{10,6},{6,2},{15,11}... | collective-permute-start | bytes 1572872 | tf_op jit(solution)/shard_map/ppermute | solution.py:198
  157.6 1.9 collective-permute-start.6
  159.6 4.1 %collective-permute-start.8 = (bf16[256,1024]{1,0:T(8,128)(2,1)}, bf16[256,1024]{1,0:T(8,128)(2,1)}, u32[]{:S(2)}, u32[]{:S(2)}) collective-permute-start(bf16[256,1024]{1,0:T(8,128)(2,1)} %collective-permute-done.3), channel_id=1, source_target_pairs={{4,8},{8,12},{5,9},{9,13},{6,10},{10,14},{7,11},{11,15},{20,24},{2... | collective-permute-start | bytes 1572872 | tf_op jit(solution)/shard_map/ppermute | solution.py:198
  163.7 2.0 collective-permute-start.9
  166.4 3.9 %collective-permute-done.7 = bf16[256,1024]{1,0:T(8,128)(2,1)S(1)} collective-permute-done((bf16[256,1024]{1,0:T(8,128)(2,1)S(1)}, bf16[256,1024]{1,0:T(8,128)(2,1)S(1)}, u32[]{:S(2)}, u32[]{:S(2)}) %collective-permute-start.7) | collective-permute-done | bytes 524320 | tf_op jit(solution)/shard_map/ppermute | solution.py:198
  170.3 1.6 collective-permute-done.6
  172.4 5.3 %collective-permute-start.14 = (bf16[256,1024]{1,0:T(8,128)(2,1)}, bf16[256,1024]{1,0:T(8,128)(2,1)}, u32[]{:S(2)}, u32[]{:S(2)}) collective-permute-start(bf16[256,1024]{1,0:T(8,128)(2,1)} %collective-permute-done.6), channel_id=1, source_target_pairs={{4,8},{8,12},{5,9},{9,13},{6,10},{10,14},{7,11},{11,15},{20,24},{2... | collective-permute-start | bytes 1572872 | tf_op jit(solution)/shard_map/ppermute | solution.py:198
  177.7 1.9 collective-permute-start.12
  179.6 7.3 %fusion.94 = (bf16[256,4608]{1,0:T(8,128)(2,1)S(1)}, f32[256,4608]{1,0:T(8,128)S(1)}) fusion(bf16[1,1536,4608]{2,1,0:T(8,128)(2,1)} %all-gather.5.cloned.1.call-done, f32[256,1536]{1,0:T(8,128)S(1)} %slice_select_fusion, f32[1536]{0:T(1024)S(1)} %get-tuple-element.65, f32[1536]{0:T(1024)S(1)} %get-tuple-element.62, f32[256]{0:T(256)S(1)} %add_rsqrt_fusion.7, ...), kind=kOutput, calls=%fused_computation.177 | convolution fusion | flops 3627024384 | bytes 22820864 | tf_op jit(solution)/shard_map/dot_general | solution.py:164
  187.6 1.5 collective-permute-start.10
  194.6 1.9 broadcast_select_fusion.5.refs_4_.refs_5_
  196.5 5.3 %collective-permute-start.16 = (bf16[256,1024]{1,0:T(8,128)(2,1)}, bf16[256,1024]{1,0:T(8,128)(2,1)}, u32[]{:S(2)}, u32[]{:S(2)}) collective-permute-start(bf16[256,1024]{1,0:T(8,128)(2,1)} %pad_maximum_fusion.7), channel_id=1, source_target_pairs={{0,4},{4,8},{1,5},{5,9},{2,6},{6,10},{3,7},{7,11},{16,20},{20,24},... | collective-permute-start | bytes 1572872 | tf_op jit(solution)/shard_map/ppermute | solution.py:198
  203.2 5.4 %collective-permute-start.13 = (bf16[256,1024]{1,0:T(8,128)(2,1)}, bf16[256,1024]{1,0:T(8,128)(2,1)}, u32[]{:S(2)}, u32[]{:S(2)}) collective-permute-start(bf16[256,1024]{1,0:T(8,128)(2,1)} %collective-permute-done.12), channel_id=1, source_target_pairs={{4,0},{5,1},{6,2},{7,3},{20,16},{21,17},{22,18},{23,19}} | collective-permute-start | bytes 1572872 | tf_op jit(solution)/shard_map/ppermute | solution.py:198
  208.5 2.0 broadcast_select_fusion.7.refs_2_.refs_3_
  214.2 4.4 %shard_map.131 = bf16[256,512]{1,0:T(8,128)(2,1)} custom-call(s32[4]{0:T(128)} %get-tuple-element.79.counts_ref, bf16[256,1536]{1,0:T(8,128)(2,1)} %copy-done.6, bf16[256,3072]{1,0:T(8,128)(2,1)} %pad_maximum_fusion.1.refs_0_.refs_1_, bf16[256,3072]{1,0:T(8,128)(2,1)} %pad_maximum_fusion.1.refs_0_.refs_1_, ...), custom_call_target="tpu_custom_call" | custom-call | flops 536870912 | bytes 2621440 | tf_op jit(solution)/shard_map/pallas_call | solution.py:93
  218.6 5.4 %collective-permute-start.17 = (bf16[256,1024]{1,0:T(8,128)(2,1)}, bf16[256,1024]{1,0:T(8,128)(2,1)S(1)}, u32[]{:S(2)}, u32[]{:S(2)}) collective-permute-start(bf16[256,1024]{1,0:T(8,128)(2,1)} %collective-permute-done.16.refs_2_.refs_3_), channel_id=1, source_target_pairs={{4,8},{5,9},{6,10},{7,11},{20,24},{21,25},{22,26},{23,27}} | collective-permute-start | bytes 1572872 | tf_op jit(solution)/shard_map/ppermute | solution.py:198
  223.9 1.9 broadcast_select_fusion.4.refs_4_.refs_5_
  226.7 4.5 %collective-permute-done.17 = bf16[256,1024]{1,0:T(8,128)(2,1)S(1)} collective-permute-done((bf16[256,1024]{1,0:T(8,128)(2,1)}, bf16[256,1024]{1,0:T(8,128)(2,1)S(1)}, u32[]{:S(2)}, u32[]{:S(2)}) %collective-permute-start.17) | collective-permute-done | bytes 524320 | tf_op jit(solution)/shard_map/ppermute | solution.py:198
  231.2 1.9 broadcast_select_fusion.3.refs_4_.refs_5_
  234.0 4.4 %shard_map.134 = bf16[256,512]{1,0:T(8,128)(2,1)} custom-call(s32[4]{0:T(128)} %pad_add_fusion.1.counts_ref, bf16[256,1536]{1,0:T(8,128)(2,1)} %copy-done.12, bf16[256,1536]{1,0:T(8,128)(2,1)} %copy-done.12, bf16[256,1536]{1,0:T(8,128)(2,1)} %copy-done.12, bf16[256,3072]{1,0:T(8,128)(2,1)} %copy-done.2, bf16[256,3072]{1,0:T(8,128)(2,1)} %copy-done.2, ...), custom_call_target="tpu_custom_call" | custom-call | flops 536870912 | bytes 2621440 | tf_op jit(solution)/shard_map/pallas_call | solution.py:93
  239.8 1.9 broadcast_select_fusion.6.refs_2_.refs_3_
  242.6 4.4 %shard_map.132 = bf16[256,512]{1,0:T(8,128)(2,1)} custom-call(s32[4]{0:T(128)} %get-tuple-element.79.counts_ref, bf16[256,1536]{1,0:T(8,128)(2,1)} %copy-done.6, bf16[256,3072]{1,0:T(8,128)(2,1)} %pad_maximum_fusion.1.refs_0_.refs_1_, bf16[256,3072]{1,0:T(8,128)(2,1)} %pad_maximum_fusion.1.refs_0_.refs_1_, ...), custom_call_target="tpu_custom_call" | custom-call | flops 536870912 | bytes 2621440 | tf_op jit(solution)/shard_map/pallas_call | solution.py:93
  246.9 4.4 %shard_map.133 = bf16[256,512]{1,0:T(8,128)(2,1)} custom-call(s32[4]{0:T(128)} %get-tuple-element.79.counts_ref, bf16[256,1536]{1,0:T(8,128)(2,1)} %copy-done.6, bf16[256,3072]{1,0:T(8,128)(2,1)} %pad_maximum_fusion.1.refs_0_.refs_1_, bf16[256,3072]{1,0:T(8,128)(2,1)} %pad_maximum_fusion.1.refs_0_.refs_1_, ...), custom_call_target="tpu_custom_call" | custom-call | flops 536870912 | bytes 2621440 | tf_op jit(solution)/shard_map/pallas_call | solution.py:93
  252.4 3.8 %fusion.95 = (f32[256]{0:T(256)S(1)}, f32[256,1536]{1,0:T(8,128)S(1)}) fusion(f32[256,1536]{1,0:T(8,128)S(1)} %slice_select_fusion, bf16[1,1536,1536]{2,1,0:T(8,128)(2,1)} %all-gather.7.cloned.1.call-done, bf16[256,512]{1,0:T(8,128)(2,1)S(1)} %broadcast_select_fusion.8, bf16[256,512]{1,0:T(8,128)(2,1)S(1)} %copy-done.24, ...), kind=kOutput, calls=%fused_computation.178 | convolution fusion | flops 1211498240 | bytes 8657920 | tf_op jit(solution)/shard_map/dot_general | solution.py:174
  256.5 1.9 collective-permute-start.23
  258.9 1.5 collective-permute-start.22
  261.9 2.6 collective-permute-done.22
  264.6 6.1 %collective-permute-done.23 = bf16[256,1536]{1,0:T(8,128)(2,1)S(1)} collective-permute-done((bf16[256,1536]{1,0:T(8,128)(2,1)S(1)}, bf16[256,1536]{1,0:T(8,128)(2,1)S(1)}, u32[]{:S(2)}, u32[]{:S(2)}) %collective-permute-start.23) | collective-permute-done | bytes 786464 | tf_op jit(solution)/shard_map/ppermute | solution.py:21
  271.2 7.4 %fusion = f32[256,4608]{1,0:T(8,128)S(1)} fusion(bf16[1,1536,4608]{2,1,0:T(8,128)(2,1)} %all-gather.5.cloned.1.call-done, bf16[256,1536]{1,0:T(8,128)(2,1)S(1)} %collective-permute-done.23, f32[256]{0:T(256)S(1)} %add_rsqrt_fusion.3, f32[256]{0:T(256)S(1)} %broadcast_multiply_fusion.1, f32[1536]{0:T(1024)S(1)} %get-tuple-element.66, ...), kind=kOutput, calls=%fused_computation | convolution fusion | flops 3626237952 | bytes 19675136 | tf_op jit(solution)/shard_map/dot_general | solution.py:164
  282.5 9.4 %shard_map.135 = bf16[256,1536]{1,0:T(8,128)(2,1)} custom-call(s32[4]{0:T(128)} %get-tuple-element.109.counts_ref, bf16[256,1536]{1,0:T(8,128)(2,1)} %get-tuple-element.82.q_ref, bf16[256,3072]{1,0:T(8,128)(2,1)} %pad_maximum_fusion.2.refs_0_.refs_1_, bf16[256,3072]{1,0:T(8,128)(2,1)} %pad_maximum_fusion.2.refs_0_.refs_1_, ...), custom_call_target="tpu_custom_call" | custom-call | flops 1610612736 | bytes 7864320 | tf_op jit(solution)/shard_map/pallas_call | solution.py:93
  291.9 4.1 %fusion.96 = (f32[256]{0:T(256)S(1)}, f32[256,1536]{1,0:T(8,128)S(1)}) fusion(bf16[256,1536]{1,0:T(8,128)(2,1)} %shard_map.135, bf16[1,1536,1536]{2,1,0:T(8,128)(2,1)} %all-gather.7.cloned.1.call-done, f32[1536]{0:T(1024)S(1)} %get-tuple-element.64, bf16[256,1536]{1,0:T(8,128)(2,1)S(1)} %collective-permute-done.23), kind=kOutput, calls=%fused_computation.179 | convolution fusion | flops 1209532160 | bytes 7871488 | tf_op jit(solution)/shard_map/dot_general | solution.py:174
  299.2 2.1 maximum_select_fusion
  (164 shorter events, 43.1 us)
Async XLA Ops:
  7.2 145.2 %copy-start = (f32[50,3072]{1,0:T(8,128)S(1)}, f32[50,3072]{1,0:T(8,128)}, u32[]{:S(2)}) copy-start(f32[50,3072]{1,0:T(8,128)} %param.21) | copy-start | bytes 1843204
  7.2 94.6 %all-gather.5.cloned.1.call-start = ((), (), s32[]{:S(2)}) async-start(), calls=%async_computation | async-start | bytes 17694720 | tf_op jit(solution)/shard_map/all_gather | solution.py:131
  7.9 133.0 %all-gather.7.cloned.1.call-start = ((), (), s32[]{:S(2)}) async-start(), calls=%async_computation.1 | async-start | bytes 5898240 | tf_op jit(solution)/shard_map/all_gather | solution.py:132
  8.7 4.9 %copy-start.26 = (s32[2,4]{1,0:T(2,128)S(1)}, s32[2,4]{1,0:T(2,128)}, u32[]{:S(2)}) copy-start(s32[2,4]{1,0:T(2,128)} %param.14) | copy-start | bytes 100
  8.7 6.0 %copy-start.27 = (f32[1,3072]{1,0:T(1,128)S(1)}, f32[1,3072]{1,0:T(1,128)}, u32[]{:S(2)}) copy-start(f32[1,3072]{1,0:T(1,128)} %param.19) | copy-start | bytes 36868
  8.7 6.0 %copy-start.16 = (f32[1,50,4608]{2,0,1:T(1,128)S(1)}, f32[1,50,4608]{2,0,1:T(1,128)}, u32[]{:S(2)}) copy-start(f32[1,50,4608]{2,0,1:T(1,128)} %param.20) | copy-start | bytes 2764804
  8.7 6.0 %copy-start.28 = (s32[2]{0:T(128)S(1)}, s32[2]{0:T(128)}, u32[]{:S(2)}) copy-start(s32[2]{0:T(128)} %param.15) | copy-start | bytes 28
  8.7 41.9 %copy-start.22 = (f32[2,1,128,64]{2,3,1,0:T(8,128)S(1)}, f32[2,1,128,64]{2,3,1,0:T(8,128)}, u32[]{:S(2)}) copy-start(f32[2,1,128,64]{2,3,1,0:T(8,128)} %param.13) | copy-start | bytes 196612
  12.0 44.3 %copy-start.2 = (bf16[256,3072]{1,0:T(8,128)(2,1)}, bf16[256,3072]{1,0:T(8,128)(2,1)S(1)}, u32[]{:S(2)}) copy-start(bf16[256,3072]{1,0:T(8,128)(2,1)S(1)} %get-tuple-element.88.refs_2_.refs_3_) | copy-start | bytes 4718596
  12.0 36.5 %collective-permute-start = (bf16[256,3072]{1,0:T(8,128)(2,1)}, bf16[256,3072]{1,0:T(8,128)(2,1)}, u32[]{:S(2)}, u32[]{:S(2)}) collective-permute-start(bf16[256,3072]{1,0:T(8,128)(2,1)} %get-tuple-element.87), channel_id=1, source_target_pairs={{0,4},{4,8},{8,12},{12,0},{1,5},{5,9},{9,13},{13,1},{2,6},{6,10},{... | collective-permute-start | bytes 4718600 | tf_op jit(solution)/shard_map/ppermute | solution.py:137
  48.5 36.5 %collective-permute-start.1 = (bf16[256,3072]{1,0:T(8,128)(2,1)}, bf16[256,3072]{1,0:T(8,128)(2,1)}, u32[]{:S(2)}, u32[]{:S(2)}) collective-permute-start(bf16[256,3072]{1,0:T(8,128)(2,1)} %collective-permute-done.refs_2_.refs_3_), channel_id=1, source_target_pairs={{0,4},{4,8},{8,12},{12,0},{1,5},{5,9},{9,13},{13,1},{2,6},{6,10},{... | collective-permute-start | bytes 4718600 | tf_op jit(solution)/shard_map/ppermute | solution.py:137
  85.0 36.7 %collective-permute-start.2 = (bf16[256,3072]{1,0:T(8,128)(2,1)}, bf16[256,3072]{1,0:T(8,128)(2,1)S(1)}, u32[]{:S(2)}, u32[]{:S(2)}) collective-permute-start(bf16[256,3072]{1,0:T(8,128)(2,1)} %collective-permute-done.1.refs_4_.refs_5_), channel_id=1, source_target_pairs={{0,4},{4,8},{8,12},{12,0},{1,5},{5,9},{9,13},{13,1},{2,6},{6,10},{... | collective-permute-start | bytes 4718600 | tf_op jit(solution)/shard_map/ppermute | solution.py:137
  112.9 18.0 %copy-start.10 = (bf16[256,1536]{1,0:T(8,128)(2,1)}, bf16[256,1536]{1,0:T(8,128)(2,1)S(1)}, u32[]{:S(2)}) copy-start(bf16[256,1536]{1,0:T(8,128)(2,1)S(1)} %get-tuple-element.85) | copy-start | bytes 2359300
  121.6 9.3 %copy-start.3 = (bf16[256,3072]{1,0:T(8,128)(2,1)}, bf16[256,3072]{1,0:T(8,128)(2,1)S(1)}, u32[]{:S(2)}) copy-start(bf16[256,3072]{1,0:T(8,128)(2,1)S(1)} %collective-permute-done.2.refs_6_.refs_7_) | copy-start | bytes 4718596
  121.6 18.7 %collective-permute-start.4 = (bf16[256,1024]{1,0:T(8,128)(2,1)}, bf16[256,1024]{1,0:T(8,128)(2,1)S(1)}, u32[]{:S(2)}, u32[]{:S(2)}) collective-permute-start(bf16[256,1024]{1,0:T(8,128)(2,1)} %get-tuple-element.23), channel_id=1, source_target_pairs={{12,8},{8,4},{4,0},{13,9},{9,5},{5,1},{14,10},{10,6},{6,2},{15,11}... | collective-permute-start | bytes 1572872 | tf_op jit(solution)/shard_map/ppermute | solution.py:198
  127.6 12.8 %collective-permute-start.3 = (bf16[256,1024]{1,0:T(8,128)(2,1)}, bf16[256,1024]{1,0:T(8,128)(2,1)}, u32[]{:S(2)}, u32[]{:S(2)}) collective-permute-start(bf16[256,1024]{1,0:T(8,128)(2,1)} %get-tuple-element.23), channel_id=1, source_target_pairs={{0,4},{4,8},{8,12},{1,5},{5,9},{9,13},{2,6},{6,10},{10,14},{3,7},{... | collective-permute-start | bytes 1572872 | tf_op jit(solution)/shard_map/ppermute | solution.py:198
  140.3 23.4 %copy-start.19 = (bf16[256,1024]{1,0:T(8,128)(2,1)}, bf16[256,1024]{1,0:T(8,128)(2,1)S(1)}, u32[]{:S(2)}) copy-start(bf16[256,1024]{1,0:T(8,128)(2,1)S(1)} %collective-permute-done.4) | copy-start | bytes 1572868
  140.9 25.3 %copy-start.5 = (f32[512,1536]{1,0:T(8,128)S(1)}, f32[512,1536]{1,0:T(8,128)}, u32[]{:S(2)}) copy-start(f32[512,1536]{1,0:T(8,128)} %copy-done.4) | copy-start | bytes 9437188
  145.5 8.2 %copy-start.21 = (bf16[256,1024]{1,0:T(8,128)(2,1)S(1)}, bf16[256,1024]{1,0:T(8,128)(2,1)}, u32[]{:S(2)}) copy-start(bf16[256,1024]{1,0:T(8,128)(2,1)} %get-tuple-element.26) | copy-start | bytes 1572868
  145.5 20.7 %collective-permute-start.5 = (bf16[256,1536]{1,0:T(8,128)(2,1)S(1)}, bf16[256,1536]{1,0:T(8,128)(2,1)S(1)}, u32[]{:S(2)}, u32[]{:S(2)}) collective-permute-start(bf16[256,1536]{1,0:T(8,128)(2,1)S(1)} %fusion.30), channel_id=1, source_target_pairs={{0,16},{1,17},{2,18},{3,19},{4,20},{5,21},{6,22},{7,23},{8,24},{9,... | collective-permute-start | bytes 2359304 | tf_op jit(solution)/shard_map/ppermute | solution.py:21
  153.6 16.7 %collective-permute-start.7 = (bf16[256,1024]{1,0:T(8,128)(2,1)S(1)}, bf16[256,1024]{1,0:T(8,128)(2,1)S(1)}, u32[]{:S(2)}, u32[]{:S(2)}) collective-permute-start(bf16[256,1024]{1,0:T(8,128)(2,1)S(1)} %copy-done.21), channel_id=1, source_target_pairs={{12,8},{8,4},{4,0},{13,9},{9,5},{5,1},{14,10},{10,6},{6,2},{15,11}... | collective-permute-start | bytes 1572872 | tf_op jit(solution)/shard_map/ppermute | solution.py:198
  157.6 14.3 %collective-permute-start.6 = (bf16[256,1024]{1,0:T(8,128)(2,1)S(1)}, bf16[256,1024]{1,0:T(8,128)(2,1)}, u32[]{:S(2)}, u32[]{:S(2)}) collective-permute-start(bf16[256,1024]{1,0:T(8,128)(2,1)S(1)} %copy-done.21), channel_id=1, source_target_pairs={{0,4},{4,8},{8,12},{1,5},{5,9},{9,13},{2,6},{6,10},{10,14},{3,7},{... | collective-permute-start | bytes 1572872 | tf_op jit(solution)/shard_map/ppermute | solution.py:198
  159.6 28.0 %collective-permute-start.8 = (bf16[256,1024]{1,0:T(8,128)(2,1)}, bf16[256,1024]{1,0:T(8,128)(2,1)}, u32[]{:S(2)}, u32[]{:S(2)}) collective-permute-start(bf16[256,1024]{1,0:T(8,128)(2,1)} %collective-permute-done.3), channel_id=1, source_target_pairs={{4,8},{8,12},{5,9},{9,13},{6,10},{10,14},{7,11},{11,15},{20,24},{2... | collective-permute-start | bytes 1572872 | tf_op jit(solution)/shard_map/ppermute | solution.py:198
  163.7 23.9 %collective-permute-start.9 = (bf16[256,1024]{1,0:T(8,128)(2,1)S(1)}, bf16[256,1024]{1,0:T(8,128)(2,1)}, u32[]{:S(2)}, u32[]{:S(2)}) collective-permute-start(bf16[256,1024]{1,0:T(8,128)(2,1)S(1)} %collective-permute-done.4), channel_id=1, source_target_pairs={{8,4},{4,0},{9,5},{5,1},{10,6},{6,2},{11,7},{7,3},{24,20},{20,16},... | collective-permute-start | bytes 1572872 | tf_op jit(solution)/shard_map/ppermute | solution.py:198
  170.3 7.3 %copy-start.17 = (bf16[256,1024]{1,0:T(8,128)(2,1)}, bf16[256,1024]{1,0:T(8,128)(2,1)S(1)}, u32[]{:S(2)}) copy-start(bf16[256,1024]{1,0:T(8,128)(2,1)S(1)} %collective-permute-done.7) | copy-start | bytes 1572868
  172.4 24.1 %collective-permute-start.14 = (bf16[256,1024]{1,0:T(8,128)(2,1)}, bf16[256,1024]{1,0:T(8,128)(2,1)}, u32[]{:S(2)}, u32[]{:S(2)}) collective-permute-start(bf16[256,1024]{1,0:T(8,128)(2,1)} %collective-permute-done.6), channel_id=1, source_target_pairs={{4,8},{8,12},{5,9},{9,13},{6,10},{10,14},{7,11},{11,15},{20,24},{2... | collective-permute-start | bytes 1572872 | tf_op jit(solution)/shard_map/ppermute | solution.py:198
  177.7 24.2 %collective-permute-start.12 = (bf16[256,1024]{1,0:T(8,128)(2,1)S(1)}, bf16[256,1024]{1,0:T(8,128)(2,1)}, u32[]{:S(2)}, u32[]{:S(2)}) collective-permute-start(bf16[256,1024]{1,0:T(8,128)(2,1)S(1)} %collective-permute-done.7), channel_id=1, source_target_pairs={{8,4},{4,0},{9,5},{5,1},{10,6},{6,2},{11,7},{7,3},{24,20},{20,16},... | collective-permute-start | bytes 1572872 | tf_op jit(solution)/shard_map/ppermute | solution.py:198
  187.6 5.9 %copy-start.6 = (bf16[256,1536]{1,0:T(8,128)(2,1)}, bf16[256,1536]{1,0:T(8,128)(2,1)S(1)}, u32[]{:S(2)}) copy-start(bf16[256,1536]{1,0:T(8,128)(2,1)S(1)} %get-tuple-element.30.q_ref) | copy-start | bytes 2359300
  187.6 6.0 %copy-start.8 = (bf16[256,1536]{1,0:T(8,128)(2,1)}, bf16[256,1536]{1,0:T(8,128)(2,1)S(1)}, u32[]{:S(2)}) copy-start(bf16[256,1536]{1,0:T(8,128)(2,1)S(1)} %get-tuple-element.83) | copy-start | bytes 2359300
  187.6 15.5 %collective-permute-start.10 = (bf16[256,1024]{1,0:T(8,128)(2,1)}, bf16[256,1024]{1,0:T(8,128)(2,1)S(1)}, u32[]{:S(2)}, u32[]{:S(2)}) collective-permute-start(bf16[256,1024]{1,0:T(8,128)(2,1)} %collective-permute-done.9), channel_id=1, source_target_pairs={{4,0},{5,1},{6,2},{7,3},{20,16},{21,17},{22,18},{23,19}} | collective-permute-start | bytes 1572872 | tf_op jit(solution)/shard_map/ppermute | solution.py:198
  189.1 22.9 %collective-permute-start.11 = (bf16[256,1024]{1,0:T(8,128)(2,1)}, bf16[256,1024]{1,0:T(8,128)(2,1)S(1)}, u32[]{:S(2)}, u32[]{:S(2)}) collective-permute-start(bf16[256,1024]{1,0:T(8,128)(2,1)} %collective-permute-done.8), channel_id=1, source_target_pairs={{8,12},{9,13},{10,14},{11,15},{24,28},{25,29},{26,30},{27,31}} | collective-permute-start | bytes 1572872 | tf_op jit(solution)/shard_map/ppermute | solution.py:198
  190.9 19.6 %collective-permute-start.18 = (bf16[256,1024]{1,0:T(8,128)(2,1)}, bf16[256,1024]{1,0:T(8,128)(2,1)S(1)}, u32[]{:S(2)}, u32[]{:S(2)}) collective-permute-start(bf16[256,1024]{1,0:T(8,128)(2,1)} %pad_maximum_fusion.7), channel_id=1, source_target_pairs={{12,8},{8,4},{13,9},{9,5},{14,10},{10,6},{15,11},{11,7},{28,24},{2... | collective-permute-start | bytes 1572872 | tf_op jit(solution)/shard_map/ppermute | solution.py:198
  194.6 18.7 %copy-start.20 = (bf16[256,1024]{1,0:T(8,128)(2,1)S(1)}, bf16[256,1024]{1,0:T(8,128)(2,1)}, u32[]{:S(2)}) copy-start(bf16[256,1024]{1,0:T(8,128)(2,1)} %copy-done.19) | copy-start | bytes 1572868
  196.5 22.1 %collective-permute-start.16 = (bf16[256,1024]{1,0:T(8,128)(2,1)}, bf16[256,1024]{1,0:T(8,128)(2,1)}, u32[]{:S(2)}, u32[]{:S(2)}) collective-permute-start(bf16[256,1024]{1,0:T(8,128)(2,1)} %pad_maximum_fusion.7), channel_id=1, source_target_pairs={{0,4},{4,8},{1,5},{5,9},{2,6},{6,10},{3,7},{7,11},{16,20},{20,24},... | collective-permute-start | bytes 1572872 | tf_op jit(solution)/shard_map/ppermute | solution.py:198
  201.8 31.2 %collective-permute-start.20 = (bf16[256,1536]{1,0:T(8,128)(2,1)}, bf16[256,1536]{1,0:T(8,128)(2,1)S(1)}, u32[]{:S(2)}, u32[]{:S(2)}) collective-permute-start(bf16[256,1536]{1,0:T(8,128)(2,1)} %pad_maximum_fusion.4), channel_id=1, source_target_pairs={{0,4},{12,8},{1,5},{13,9},{2,6},{14,10},{3,7},{15,11},{16,20},{28,... | collective-permute-start | bytes 2359304 | tf_op jit(solution)/shard_map/ppermute | solution.py:198
  203.2 36.6 %collective-permute-start.13 = (bf16[256,1024]{1,0:T(8,128)(2,1)}, bf16[256,1024]{1,0:T(8,128)(2,1)}, u32[]{:S(2)}, u32[]{:S(2)}) collective-permute-start(bf16[256,1024]{1,0:T(8,128)(2,1)} %collective-permute-done.12), channel_id=1, source_target_pairs={{4,0},{5,1},{6,2},{7,3},{20,16},{21,17},{22,18},{23,19}} | collective-permute-start | bytes 1572872 | tf_op jit(solution)/shard_map/ppermute | solution.py:198
  210.5 15.3 %copy-start.13 = (bf16[256,1024]{1,0:T(8,128)(2,1)}, bf16[256,1024]{1,0:T(8,128)(2,1)S(1)}, u32[]{:S(2)}) copy-start(bf16[256,1024]{1,0:T(8,128)(2,1)S(1)} %collective-permute-done.18.refs_6_.refs_7_) | copy-start | bytes 1572868
  210.5 31.2 %collective-permute-start.15 = (bf16[256,1024]{1,0:T(8,128)(2,1)}, bf16[256,1024]{1,0:T(8,128)(2,1)}, u32[]{:S(2)}, u32[]{:S(2)}) collective-permute-start(bf16[256,1024]{1,0:T(8,128)(2,1)} %collective-permute-done.14), channel_id=1, source_target_pairs={{8,12},{9,13},{10,14},{11,15},{24,28},{25,29},{26,30},{27,31}} | collective-permute-start | bytes 1572872 | tf_op jit(solution)/shard_map/ppermute | solution.py:198
  212.0 14.7 %collective-permute-start.19 = (bf16[256,1024]{1,0:T(8,128)(2,1)S(1)}, bf16[256,1024]{1,0:T(8,128)(2,1)}, u32[]{:S(2)}, u32[]{:S(2)}) collective-permute-start(bf16[256,1024]{1,0:T(8,128)(2,1)S(1)} %collective-permute-done.18.refs_6_.refs_7_), channel_id=1, source_target_pairs={{8,4},{9,5},{10,6},{11,7},{24,20},{25,21},{26,22},{27,23}} | collective-permute-start | bytes 1572872 | tf_op jit(solution)/shard_map/ppermute | solution.py:198
  218.6 12.6 %collective-permute-start.17 = (bf16[256,1024]{1,0:T(8,128)(2,1)}, bf16[256,1024]{1,0:T(8,128)(2,1)S(1)}, u32[]{:S(2)}, u32[]{:S(2)}) collective-permute-start(bf16[256,1024]{1,0:T(8,128)(2,1)} %collective-permute-done.16.refs_2_.refs_3_), channel_id=1, source_target_pairs={{4,8},{5,9},{6,10},{7,11},{20,24},{21,25},{22,26},{23,27}} | collective-permute-start | bytes 1572872 | tf_op jit(solution)/shard_map/ppermute | solution.py:198
  238.4 3.4 %copy-start.18 = (bf16[256,1024]{1,0:T(8,128)(2,1)S(1)}, bf16[256,1024]{1,0:T(8,128)(2,1)}, u32[]{:S(2)}) copy-start(bf16[256,1024]{1,0:T(8,128)(2,1)} %copy-done.17) | copy-start | bytes 1572868
  238.4 13.0 %collective-permute-start.21 = (bf16[256,512]{1,0:T(8,128)(2,1)}, bf16[256,512]{1,0:T(8,128)(2,1)S(1)}, u32[]{:S(2)}, u32[]{:S(2)}) collective-permute-start(bf16[256,512]{1,0:T(8,128)(2,1)} %shard_map.134), channel_id=1, source_target_pairs={{4,0},{8,12},{5,1},{9,13},{6,2},{10,14},{7,3},{11,15},{20,16},{24,... | collective-permute-start | bytes 786440 | tf_op jit(solution)/shard_map/ppermute | solution.py:198
  246.9 5.4 %copy-start.23 = (bf16[256,512]{1,0:T(8,128)(2,1)S(1)}, bf16[256,512]{1,0:T(8,128)(2,1)}, u32[]{:S(2)}) copy-start(bf16[256,512]{1,0:T(8,128)(2,1)} %shard_map.131) | copy-start | bytes 786436
  246.9 5.4 %copy-start.24 = (bf16[256,512]{1,0:T(8,128)(2,1)S(1)}, bf16[256,512]{1,0:T(8,128)(2,1)}, u32[]{:S(2)}) copy-start(bf16[256,512]{1,0:T(8,128)(2,1)} %shard_map.132) | copy-start | bytes 786436
  256.5 14.1 %collective-permute-start.23 = (bf16[256,1536]{1,0:T(8,128)(2,1)S(1)}, bf16[256,1536]{1,0:T(8,128)(2,1)S(1)}, u32[]{:S(2)}, u32[]{:S(2)}) collective-permute-start(bf16[256,1536]{1,0:T(8,128)(2,1)S(1)} %get-tuple-element.94), channel_id=1, source_target_pairs={{0,16},{1,17},{2,18},{3,19},{4,20},{5,21},{6,22},{7,23},{8,24},{9,... | collective-permute-start | bytes 2359304 | tf_op jit(solution)/shard_map/ppermute | solution.py:21
  258.9 5.6 %collective-permute-start.22 = (bf16[128,64]{0,1:T(8,128)(2,1)S(1)}, bf16[128,64]{0,1:T(8,128)(2,1)S(1)}, u32[]{:S(2)}, u32[]{:S(2)}) collective-permute-start(bf16[128,64]{0,1:T(8,128)(2,1)S(1)} %slice.273), channel_id=1, source_target_pairs={{16,0},{17,1},{18,2},{19,3},{20,4},{21,5},{22,6},{23,7},{24,8},{25... | collective-permute-start | bytes 49160 | tf_op jit(solution)/shard_map/ppermute | solution.py:21
  296.8 5.8 %collective-permute-start.24 = (bf16[128,64]{0,1:T(8,128)(2,1)S(1)}, bf16[128,64]{0,1:T(8,128)(2,1)S(1)}, u32[]{:S(2)}, u32[]{:S(2)}) collective-permute-start(bf16[128,64]{0,1:T(8,128)(2,1)S(1)} %slice.272), channel_id=1, source_target_pairs={{16,0},{17,1},{18,2},{19,3},{20,4},{21,5},{22,6},{23,7},{24,8},{25... | collective-permute-start | bytes 49160 | tf_op jit(solution)/shard_map/ppermute | solution.py:21
  299.2 4.8 %copy-start.1 = (f32[50,3072]{1,0:T(8,128)S(1)}, f32[50,3072]{1,0:T(8,128)}, u32[]{:S(2)}) copy-start(f32[50,3072]{1,0:T(8,128)} %param.21) | copy-start | bytes 1843204
  (9 other events, 17.3 us)
Sparse Core Ops, SparseCore 0:
  9.6 92.1 all-gather.4
  103.4 37.4 all-gather.6

commit v3 on v1

--- a/solution.py
+++ b/solution.py
@@ -45,6 +45,8 @@
 def attend_kernel(counts_ref, q_ref, *refs):
     blocks = (len(refs) - 1) // 2
     out_ref = refs[-1]
+    slot = lax.broadcasted_iota(jnp.int32, (1, refs[0].shape[0]), 1)
+    bias = [jnp.where(slot < counts_ref[b], 0.0, -jnp.inf) for b in range(blocks)]
     for head in range(q_ref.shape[1] // HD):
         cols = slice(head * HD, (head + 1) * HD)
         query = q_ref[:, cols]
@@ -52,9 +54,8 @@
         for b in range(blocks):
             score = lax.dot_general(
                 query, refs[2 * b][:, cols], (((1,), (1,)), ((), ())), preferred_element_type=jnp.float32
-            ) * (1.0 / math.sqrt(HD))
-            slot = lax.broadcasted_iota(jnp.int32, score.shape, 1)
-            scores.append(jnp.where(slot < counts_ref[b], score, -jnp.inf))
+            )
+            scores.append(score * (math.log2(math.e) / math.sqrt(HD)) + bias[b])
         top = scores[0]
         for score in scores[1:]:
             top = jnp.maximum(top, score)
@@ -62,7 +63,7 @@
         total = None
         mixed = None
         for b in range(blocks):
-            weight = jnp.exp(scores[b] - top)
+            weight = jnp.exp2(scores[b] - top)
             part = jnp.dot(
                 weight.astype(jnp.bfloat16), refs[2 * b + 1][:, cols], preferred_element_type=jnp.float32
             )
@@ -72,27 +73,32 @@
         out_ref[:, cols] = (mixed / denom).astype(jnp.bfloat16)
 
 
-def attend(queries, kv_blocks, block_counts):
-    rows, model_width = queries.shape
+def attend(heads, queries, q_head, kv_blocks, block_counts):
+    rows = queries.shape[0]
     cols = HEADS_STEP * HD
-    steps = model_width // cols
-    specs = [pl.BlockSpec(memory_space=pltpu.SMEM), pl.BlockSpec((rows, cols), lambda h: (0, h))]
+    steps = heads // HEADS_STEP
+
+    def spec(array, first_head):
+        first = first_head // HEADS_STEP
+        return pl.BlockSpec((array.shape[0], cols), lambda h: (0, h + first))
+
+    specs = [pl.BlockSpec(memory_space=pltpu.SMEM), spec(queries, q_head)]
     operands = [block_counts, queries]
-    for kv in kv_blocks:
-        specs.append(pl.BlockSpec((kv.shape[0], cols), lambda h: (0, h)))
-        specs.append(pl.BlockSpec((kv.shape[0], cols), lambda h: (0, h + steps)))
-        operands += [kv, kv]
-    keys = sum(kv.shape[0] for kv in kv_blocks)
+    for keys, key_head, values, value_head in kv_blocks:
+        specs += [spec(keys, key_head), spec(values, value_head)]
+        operands += [keys, values]
+    keys = rows * len(kv_blocks)
+    width = heads * HD
     return pl.pallas_call(
         attend_kernel,
         grid=(steps,),
         in_specs=specs,
         out_specs=pl.BlockSpec((rows, cols), lambda h: (0, h)),
-        out_shape=jax.ShapeDtypeStruct((rows, model_width), jnp.bfloat16),
+        out_shape=jax.ShapeDtypeStruct((rows, width), jnp.bfloat16),
         cost_estimate=pl.CostEstimate(
-            flops=4 * rows * keys * model_width,
-            bytes_accessed=4 * (rows + keys) * model_width,
-            transcendentals=rows * keys * HEADS,
+            flops=4 * rows * keys * width,
+            bytes_accessed=4 * (rows + keys) * width,
+            transcendentals=rows * keys * heads,
         ),
     )(*operands)
 
@@ -114,7 +120,7 @@
     own_patch = lax.axis_index("patch")
     first_section = section_index == 0
     videos = latent.shape[0]
-    assert videos == 2 and lax.axis_size("section") == 2
+    assert videos == 2 and lax.axis_size("section") == 2 and counts.shape[1] == 4
     patch_rows = stale_cache.shape[3]
     model_width = embed_weight.shape[1]
     patch_count = counts.shape[1]
@@ -125,18 +131,27 @@
     out_full = lax.all_gather(wo[0], "fsdp", axis=0, tiled=True)
     ring = [(i, (i + 1) % patch_count) for i in range(patch_count)]
 
-    def around(video, after=None):
-        block = lax.dynamic_index_in_dim(stale_cache[0, :, 0], video, 0, keepdims=False)
-        if after is not None:
-            block, _ = lax.optimization_barrier((block, after))
-        blocks = []
-        for _ in range(patch_count - 1):
-            block = lax.ppermute(block, "patch", ring)
-            blocks.append(block)
-        return blocks
-
-    early_blocks = around(early)
-    late_blocks = around(late, early_blocks[-1])
+    def after(value, *earlier):
+        return lax.optimization_barrier((value,) + earlier)[0]
+
+    def step(block):
+        return lax.ppermute(block, "patch", ring)
+
+    def across(block, to_first):
+        return lax.ppermute(block, "section", [(1, 0)] if to_first else [(0, 1)])
+
+    early_stale = lax.dynamic_index_in_dim(stale_cache[0, :, 0], early, 0, keepdims=False)
+    late_stale = lax.dynamic_index_in_dim(stale_cache[0, :, 0], late, 0, keepdims=False)
+    early_keys, early_values = early_stale[:, :model_width], early_stale[:, model_width:]
+    first_mix = jnp.where(first_section, early_keys, across(early_values, False))
+    last_mix = jnp.where(first_section, across(early_values, True), early_keys)
+    late_1 = step(late_stale)
+    first_keys, first_values = [], []
+    block = after(first_mix, late_1)
+    for _ in range(patch_count - 1):
+        block = step(block)
+        first_keys.append(block)
+        first_values.append(across(block, True))
 
     start_hidden = jnp.dot(
         rows_full.reshape(-1, rows_full.shape[3]), embed_weight, preferred_element_type=jnp.float32
@@ -154,12 +169,13 @@
     )
     own_live = slot_iota[None, :] < ring_counts[:, :1]
 
-    def layer(hidden, video, stale_blocks):
+    def counts_of(video):
+        return lax.dynamic_index_in_dim(ring_counts, video, 0, keepdims=False)
+
+    def project(hidden, video):
         mod = lax.dynamic_index_in_dim(modulation_all, video, 0)
-        block_counts = lax.dynamic_index_in_dim(ring_counts, video, 0, keepdims=False)
         shift_vec = mod[:, :model_width]
         scale_vec = mod[:, model_width : 2 * model_width]
-        gate_vec = mod[:, 2 * model_width :]
         normed = (layer_norm(hidden) * (1.0 + scale_vec) + shift_vec).astype(jnp.bfloat16)
         projected = jnp.dot(normed, proj_full, preferred_element_type=jnp.float32)
         queries = rms_norm(projected[:, :model_width], gain_rows[:model_width]).astype(jnp.bfloat16)
@@ -167,9 +183,17 @@
         fresh_kv = jnp.concatenate(
             [keys.astype(jnp.bfloat16), projected[:, 2 * model_width :].astype(jnp.bfloat16)], axis=-1
         )
-        attended = attend(queries, [fresh_kv] + stale_blocks, block_counts)
-        update = jnp.dot(attended, out_full, preferred_element_type=jnp.float32)
-        return hidden + gate_vec * update, fresh_kv
+        return queries, fresh_kv
+
+    def finish(hidden, attended, video):
+        gate_vec = lax.dynamic_index_in_dim(modulation_all, video, 0)[:, 2 * model_width :]
+        return hidden + gate_vec * jnp.dot(attended, out_full, preferred_element_type=jnp.float32)
+
+    def attend_with(queries, fresh_kv, keys, values, video):
+        blocks = [(fresh_kv, 0, fresh_kv, HEADS)]
+        for key, value in zip(keys, values):
+            blocks.append((key, 0, value, value.shape[1] // HD - HEADS))
+        return attend(HEADS, queries, 0, blocks, counts_of(video))
 
     def head(hidden, video):
         head_in = (
@@ -185,12 +209,28 @@
     def forward(hidden):
         return shifted(hidden.astype(jnp.bfloat16), "section", 1).astype(jnp.float32)
 
-    hidden_a, fresh_a = layer(start_hidden[0], early, early_blocks)
+    queries_a, fresh_a = project(start_hidden[0], early)
+    late_2 = step(after(late_1, first_keys[-1]))
+    attended_a = attend_with(queries_a, fresh_a, first_keys, first_values, early)
+    late_3 = step(late_2)
+    hidden_a = finish(start_hidden[0], attended_a, early)
     received = forward(hidden_a)
-    hidden_b, fresh_b = layer(jnp.where(first_section, start_hidden[1], received), late, late_blocks)
+    hidden_b = jnp.where(first_section, start_hidden[1], received)
+    queries_b, fresh_b = project(hidden_b, late)
+    last_keys, last_values = [], []
+    block = after(last_mix, late_3)
+    for _ in range(patch_count - 1):
+        block = step(block)
+        last_keys.append(block)
+        last_values.append(across(block, False))
+    late_blocks = [late_1, late_2, late_3]
+    attended_b = attend_with(queries_b, fresh_b, late_blocks, late_blocks, late)
+    hidden_b = finish(hidden_b, attended_b, late)
     received = forward(hidden_b)
     first_half = head(hidden_b, 0)
-    hidden_c, fresh_c = layer(received, early, early_blocks)
+    queries_c, fresh_c = project(received, early)
+    attended_c = attend_with(queries_c, fresh_c, last_keys, last_values, early)
+    hidden_c = finish(received, attended_c, early)
     second_half = head(hidden_c, 1)
     cache_buf = jnp.stack(
         [jnp.where(first_section, fresh_a, fresh_b), jnp.where(first_section, fresh_b, fresh_c)]

time: 299 us -> 380 us (1.27)
  waiting for transfers between devices: 170 us -> 232 us
  starting transfers between devices: 11.7 us -> 27.6 us
    ppermute x6 -> x17, waiting for transfers between devices: 155 us -> 198 us  [the longest x9 159 us: step(): return lax.ppermute(block, 'patch', ring)]
    ppermute x4, waiting for transfers between devices: 13.6 us -> 32.6 us  [shifted(): return lax.ppermute(shard, axis, pairs)]
    ppermute x6 -> x17, starting transfers between devices: 3.09 us -> 19 us  [the longest x8 16 us: across(): return lax.ppermute(block, 'section', [(1, 0)] if to_first else [(0, 1)])]
  transfers between devices with their start and end apart: 12 -> 23, of which waited for: 10 -> 16; matrix products, arithmetic and copies ran while one was open for 14% -> 16% of each run, Pallas kernels for 3% -> 5%
where the time goes in v3:
time: 380 us; the launch traced here: 379 us
  waiting for transfers between devices  232 us (61%)
  matrix products  38.4 us (10%)
  Pallas kernels  28.2 us (7%)
  starting transfers between devices  27.6 us (7%)
  other arithmetic  19.1 us (5%)
  local copies, waits for them, and re-layouts  14.7 us (4%)
  between operations  14.6 us (4%)
  blocking collectives  4.61 us (1%)
    ppermute x9, waiting for transfers between devices, step(): return lax.ppermute(block, 'patch', ring)  159 us
    ppermute x8, waiting for transfers between devices, across(): return lax.ppermute(block, 'section', [(1, 0)] if to_first else [(0, 1)])  39.6 us
    ppermute x4, waiting for transfers between devices, shifted(): return lax.ppermute(shard, axis, pairs)  32.6 us
    pallas_call x3, Pallas kernels, attend(): pl.pallas_call(attend_kernel, grid=(steps,), in_specs=specs, out_specs=pl...  28.2 us
    dot_general x3, matrix products, project(): projected = jnp.dot(normed, proj_full, preferred_element_type=jnp.float32)  22.6 us
    ppermute x8, starting transfers between devices, across(): return lax.ppermute(block, 'section', [(1, 0)] if to_first else [(0, 1)])  16 us
    dot_general x3, matrix products, finish(): jnp.dot(attended, out_full, preferred_element_type=jnp.float32)  13.4 us
    ppermute x4, starting transfers between devices, shifted(): return lax.ppermute(shard, axis, pairs)  8.52 us
  transfers between devices with their start and end apart: 23, of which 16 were waited for; matrix products, arithmetic and copies ran while one was open for 16% of the time, Pallas kernels for 5%

profile of v3, /device:TPU:0, one launch (start us, length us, event | category | flops | bytes accessed | tf_op | source)
XLA Modules:
  0.0 378.8 jit_solution(2737187659671174603)
XLA Ops:
  8.0 3.2 dynamic-slice_bitcast_fusion
  11.2 3.0 collective-permute-start.1
  14.3 4.3 %collective-permute-start = (bf16[256,1536]{1,0:T(8,128)(2,1)S(1)}, bf16[256,1536]{1,0:T(8,128)(2,1)}, u32[]{:S(2)}, u32[]{:S(2)}) collective-permute-start(bf16[256,1536]{1,0:T(8,128)(2,1)S(1)} %slice.155), channel_id=1, source_target_pairs={{0,16},{1,17},{2,18},{3,19},{4,20},{5,21},{6,22},{7,23},{8,24},{9,... | collective-permute-start | bytes 2359304 | tf_op jit(solution)/shard_map/ppermute | solution.py:141
  19.9 14.3 %collective-permute-done = bf16[256,1536]{1,0:T(8,128)(2,1)} collective-permute-done((bf16[256,1536]{1,0:T(8,128)(2,1)S(1)}, bf16[256,1536]{1,0:T(8,128)(2,1)}, u32[]{:S(2)}, u32[]{:S(2)}) %collective-permute-start) | collective-permute-done | bytes 786464 | tf_op jit(solution)/shard_map/ppermute | solution.py:141
  34.2 5.1 %collective-permute-done.13 = bf16[256,1536]{1,0:T(8,128)(2,1)} collective-permute-done((bf16[256,1536]{1,0:T(8,128)(2,1)S(1)}, bf16[256,1536]{1,0:T(8,128)(2,1)}, u32[]{:S(2)}, u32[]{:S(2)}) %collective-permute-start.13) | collective-permute-done | bytes 786464 | tf_op jit(solution)/shard_map/ppermute | solution.py:141
  39.3 2.1 broadcast_select_fusion
  41.4 9.5 %collective-permute-done.1.refs_2_.refs_3_ = bf16[256,3072]{1,0:T(8,128)(2,1)} collective-permute-done((bf16[256,3072]{1,0:T(8,128)(2,1)}, bf16[256,3072]{1,0:T(8,128)(2,1)}, u32[]{:S(2)}, u32[]{:S(2)}) %collective-permute-start.1) | collective-permute-done | bytes 1572896 | tf_op jit(solution)/shard_map/ppermute | solution.py:138
  51.0 20.5 %collective-permute-done.2.refs_2_ = bf16[256,1536]{1,0:T(8,128)(2,1)S(1)} collective-permute-done((bf16[256,1536]{1,0:T(8,128)(2,1)S(1)}, bf16[256,1536]{1,0:T(8,128)(2,1)S(1)}, u32[]{:S(2)}, u32[]{:S(2)}) %collective-permute-start.2) | collective-permute-done | bytes 786464 | tf_op jit(solution)/shard_map/ppermute | solution.py:138
  71.5 19.6 %collective-permute-done.4.refs_4_ = bf16[256,1536]{1,0:T(8,128)(2,1)S(1)} collective-permute-done((bf16[256,1536]{1,0:T(8,128)(2,1)S(1)}, bf16[256,1536]{1,0:T(8,128)(2,1)S(1)}, u32[]{:S(2)}, u32[]{:S(2)}) %collective-permute-start.4) | collective-permute-done | bytes 786464 | tf_op jit(solution)/shard_map/ppermute | solution.py:138
  92.0 17.9 %collective-permute-done.6.refs_6_ = bf16[256,1536]{1,0:T(8,128)(2,1)} collective-permute-done((bf16[256,1536]{1,0:T(8,128)(2,1)S(1)}, bf16[256,1536]{1,0:T(8,128)(2,1)}, u32[]{:S(2)}, u32[]{:S(2)}) %collective-permute-start.6) | collective-permute-done | bytes 786464 | tf_op jit(solution)/shard_map/ppermute | solution.py:138
  109.9 34.8 %collective-permute-done.9.refs_4_.refs_5_ = bf16[256,3072]{1,0:T(8,128)(2,1)S(1)} collective-permute-done((bf16[256,3072]{1,0:T(8,128)(2,1)}, bf16[256,3072]{1,0:T(8,128)(2,1)S(1)}, u32[]{:S(2)}, u32[]{:S(2)}) %collective-permute-start.9) | collective-permute-done | bytes 1572896 | tf_op jit(solution)/shard_map/ppermute | solution.py:138
  144.7 4.6 %all_gather.9 = bf16[2,1,256,64]{2,3,1,0:T(8,128)(2,1)S(1)} all-gather(bf16[2,1,128,64]{2,3,1,0:T(8,128)(2,1)S(1)} %convert_element_type.63), channel_id=1, replica_groups=mesh['section'=2,'patch'=4,'fsdp'=4] {'section'}, dimensions={2}, use_global_device_ids=true | all-gather | bytes 98304 | tf_op jit(solution)/shard_map/all_gather | solution.py:129
  150.5 28.8 %collective-permute-done.10.refs_6_.refs_7_ = bf16[256,3072]{1,0:T(8,128)(2,1)} collective-permute-done((bf16[256,3072]{1,0:T(8,128)(2,1)S(1)}, bf16[256,3072]{1,0:T(8,128)(2,1)}, u32[]{:S(2)}, u32[]{:S(2)}) %collective-permute-start.10) | collective-permute-done | bytes 1572896 | tf_op jit(solution)/shard_map/ppermute | solution.py:138
  180.2 16.6 %collective-permute-done.14.refs_2_ = bf16[256,1536]{1,0:T(8,128)(2,1)} collective-permute-done((bf16[256,1536]{1,0:T(8,128)(2,1)S(1)}, bf16[256,1536]{1,0:T(8,128)(2,1)}, u32[]{:S(2)}, u32[]{:S(2)}) %collective-permute-start.14) | collective-permute-done | bytes 786464 | tf_op jit(solution)/shard_map/ppermute | solution.py:138
  197.7 1.7 multiply_reduce_fusion.9
  199.5 1.3 collective-permute-start.3
  200.8 1.3 collective-permute-start.5
  202.1 1.3 collective-permute-start.7
  203.4 11.0 %collective-permute-done.16.refs_4_ = bf16[256,1536]{1,0:T(8,128)(2,1)} collective-permute-done((bf16[256,1536]{1,0:T(8,128)(2,1)}, bf16[256,1536]{1,0:T(8,128)(2,1)}, u32[]{:S(2)}, u32[]{:S(2)}) %collective-permute-start.16) | collective-permute-done | bytes 786464 | tf_op jit(solution)/shard_map/ppermute | solution.py:138
  214.5 7.7 %fusion.4 = f32[256,4608]{1,0:T(8,128)S(1)} fusion(bf16[1,1536,4608]{2,1,0:T(8,128)(2,1)} %all-gather.5.cloned.1.call-done, f32[512,1536]{1,0:T(8,128)} %copy-done.2, f32[1536]{0:T(1024)S(1)} %get-tuple-element.38, f32[1536]{0:T(1024)S(1)} %get-tuple-element.35, f32[256]{0:T(256)S(1)} %add_rsqrt_fusion.10, f32[256]{0:T(256)S(1)} %broadcast_multiply_fusion.4), kind=kOutput, calls=%fused_computation.4 | convolution fusion | flops 3625844736 | bytes 20461568 | tf_op jit(solution)/shard_map/dot_general | solution.py:180
  222.6 1.8 copy-done.4
  225.6 1.4 pad_maximum_fusion.refs_0_.refs_1_
  227.0 11.7 %collective-permute-done.5.refs_5_ = bf16[256,1536]{1,0:T(8,128)(2,1)} collective-permute-done((bf16[256,1536]{1,0:T(8,128)(2,1)S(1)}, bf16[256,1536]{1,0:T(8,128)(2,1)}, u32[]{:S(2)}, u32[]{:S(2)}) %collective-permute-start.5) | collective-permute-done | bytes 786464 | tf_op jit(solution)/shard_map/ppermute | solution.py:141
  238.7 8.4 %collective-permute-done.7.refs_7_ = bf16[256,1536]{1,0:T(8,128)(2,1)} collective-permute-done((bf16[256,1536]{1,0:T(8,128)(2,1)}, bf16[256,1536]{1,0:T(8,128)(2,1)}, u32[]{:S(2)}, u32[]{:S(2)}) %collective-permute-start.7) | collective-permute-done | bytes 786464 | tf_op jit(solution)/shard_map/ppermute | solution.py:141
  247.1 9.4 %shard_map.130 = bf16[256,1536]{1,0:T(8,128)(2,1)} custom-call(s32[4]{0:T(128)} %get-tuple-element.46.counts_ref, bf16[256,1536]{1,0:T(8,128)(2,1)} %get-tuple-element.58.q_ref, bf16[256,3072]{1,0:T(8,128)(2,1)} %pad_maximum_fusion.refs_0_.refs_1_, bf16[256,3072]{1,0:T(8,128)(2,1)} %pad_maximum_fusion.refs_0_.refs_1_, bf16[256,1536]{1,0:T(8,128)(2,1)} %copy-done.12, ...), custom_call_target="tpu_custom_call" | custom-call | flops 1610612736 | bytes 7864320 | tf_op jit(solution)/shard_map/pallas_call | solution.py:92
  256.5 4.6 %fusion.30 = bf16[256,1536]{1,0:T(8,128)(2,1)S(1)} fusion(bf16[256,1536]{1,0:T(8,128)(2,1)} %shard_map.130, bf16[1,1536,1536]{2,1,0:T(8,128)(2,1)} %all-gather.7.cloned.1.call-done, f32[512,1536]{1,0:T(8,128)} %copy-done.2, f32[1536]{0:T(1024)S(1)} %get-tuple-element.36), kind=kOutput, calls=%fused_computation.19 | convolution fusion | flops 1209139200 | bytes 7870464 | tf_op jit(solution)/shard_map/dot_general | solution.py:190
  261.1 1.5 collective-permute-start.8
  262.6 2.2 collective-permute-start.15
  264.8 2.2 collective-permute-start.17
  267.0 2.2 collective-permute-start.19
  269.2 2.4 slice_bitcast_fusion
  271.6 8.9 %collective-permute-done.8 = bf16[256,1536]{1,0:T(8,128)(2,1)S(1)} collective-permute-done((bf16[256,1536]{1,0:T(8,128)(2,1)S(1)}, bf16[256,1536]{1,0:T(8,128)(2,1)S(1)}, u32[]{:S(2)}, u32[]{:S(2)}) %collective-permute-start.8) | collective-permute-done | bytes 786464 | tf_op jit(solution)/shard_map/ppermute | solution.py:21
  281.2 7.5 %fusion.2 = f32[256,4608]{1,0:T(8,128)S(1)} fusion(bf16[1,1536,4608]{2,1,0:T(8,128)(2,1)} %all-gather.5.cloned.1.call-done, f32[1536]{0:T(1024)S(1)} %get-tuple-element.37, f32[1536]{0:T(1024)S(1)} %get-tuple-element.34, f32[256]{0:T(256)S(1)} %add_rsqrt_fusion.7, f32[256]{0:T(256)S(1)} %broadcast_multiply_fusion.3, f32[512,1536]{1,0:T(8,128)S(1)} %copy-done.3, ...), kind=kOutput, calls=%fused_computation.2 | convolution fusion | flops 3626631168 | bytes 21252096 | tf_op jit(solution)/shard_map/dot_general | solution.py:180
  289.1 1.8 copy-done.5
  292.0 1.4 pad_maximum_fusion.1.refs_0_.refs_1_
  293.4 9.4 %shard_map.131 = bf16[256,1536]{1,0:T(8,128)(2,1)} custom-call(s32[4]{0:T(128)} %get-tuple-element.45.counts_ref, bf16[256,1536]{1,0:T(8,128)(2,1)} %get-tuple-element.56.q_ref, bf16[256,3072]{1,0:T(8,128)(2,1)} %pad_maximum_fusion.1.refs_0_.refs_1_, bf16[256,3072]{1,0:T(8,128)(2,1)} %pad_maximum_fusion.1.refs_0_.refs_1_, ...), custom_call_target="tpu_custom_call" | custom-call | flops 1610612736 | bytes 7864320 | tf_op jit(solution)/shard_map/pallas_call | solution.py:92
  302.8 4.6 %fusion.86 = (f32[256]{0:T(256)S(1)}, f32[256,1536]{1,0:T(8,128)S(1)}) fusion(bf16[256,1536]{1,0:T(8,128)(2,1)} %shard_map.131, bf16[1,1536,1536]{2,1,0:T(8,128)(2,1)} %all-gather.7.cloned.1.call-done, f32[1536]{0:T(1024)S(1)} %get-tuple-element.33, bf16[256,1536]{1,0:T(8,128)(2,1)S(1)} %collective-permute-done.8, f32[512,1536]{1,0:T(8,128)} %copy-done.2, ...), kind=kOutput, calls=%fused_computation.157 | convolution fusion | flops 1209925376 | bytes 9444353 | tf_op jit(solution)/shard_map/dot_general | solution.py:190
  307.7 4.4 %collective-permute-start.12 = (bf16[256,1536]{1,0:T(8,128)(2,1)S(1)}, bf16[256,1536]{1,0:T(8,128)(2,1)S(1)}, u32[]{:S(2)}, u32[]{:S(2)}) collective-permute-start(bf16[256,1536]{1,0:T(8,128)(2,1)S(1)} %get-tuple-element.64), channel_id=1, source_target_pairs={{0,16},{1,17},{2,18},{3,19},{4,20},{5,21},{6,22},{7,23},{8,24},{9,... | collective-permute-start | bytes 2359304 | tf_op jit(solution)/shard_map/ppermute | solution.py:21
  312.6 1.3 collective-permute-start.11
  313.9 2.4 slice_bitcast_fusion.1
  316.3 1.9 collective-permute-done.11
  318.3 20.3 %collective-permute-done.12 = bf16[256,1536]{1,0:T(8,128)(2,1)S(1)} collective-permute-done((bf16[256,1536]{1,0:T(8,128)(2,1)S(1)}, bf16[256,1536]{1,0:T(8,128)(2,1)S(1)}, u32[]{:S(2)}, u32[]{:S(2)}) %collective-permute-start.12) | collective-permute-done | bytes 786464 | tf_op jit(solution)/shard_map/ppermute | solution.py:21
  339.1 7.4 %fusion = f32[256,4608]{1,0:T(8,128)S(1)} fusion(bf16[1,1536,4608]{2,1,0:T(8,128)(2,1)} %all-gather.5.cloned.1.call-done, bf16[256,1536]{1,0:T(8,128)(2,1)S(1)} %collective-permute-done.12, f32[256]{0:T(256)S(1)} %add_rsqrt_fusion.3, f32[256]{0:T(256)S(1)} %broadcast_multiply_fusion.1, f32[1536]{0:T(1024)S(1)} %get-tuple-element.38, ...), kind=kOutput, calls=%fused_computation | convolution fusion | flops 3626237952 | bytes 19675136 | tf_op jit(solution)/shard_map/dot_general | solution.py:180
  348.1 1.4 pad_maximum_fusion.2.refs_0_.refs_1_
  350.4 9.4 %shard_map.132 = bf16[256,1536]{1,0:T(8,128)(2,1)} custom-call(s32[4]{0:T(128)} %get-tuple-element.46.counts_ref, bf16[256,1536]{1,0:T(8,128)(2,1)} %get-tuple-element.54.q_ref, bf16[256,3072]{1,0:T(8,128)(2,1)} %pad_maximum_fusion.2.refs_0_.refs_1_, bf16[256,3072]{1,0:T(8,128)(2,1)} %pad_maximum_fusion.2.refs_0_.refs_1_, ...), custom_call_target="tpu_custom_call" | custom-call | flops 1610612736 | bytes 7864320 | tf_op jit(solution)/shard_map/pallas_call | solution.py:92
  359.8 4.3 %fusion.87 = (f32[256]{0:T(256)S(1)}, f32[256,1536]{1,0:T(8,128)S(1)}) fusion(bf16[256,1536]{1,0:T(8,128)(2,1)} %shard_map.132, bf16[1,1536,1536]{2,1,0:T(8,128)(2,1)} %all-gather.7.cloned.1.call-done, f32[1536]{0:T(1024)S(1)} %get-tuple-element.36, bf16[256,1536]{1,0:T(8,128)(2,1)} %copy-done.7), kind=kOutput, calls=%fused_computation.158 | convolution fusion | flops 1209532160 | bytes 7871488 | tf_op jit(solution)/shard_map/dot_general | solution.py:190
  367.1 2.1 maximum_select_fusion
  369.2 1.4 collective-permute-done.20
  (120 shorter events, 18.0 us)
Async XLA Ops:
  7.2 172.2 %copy-start = (f32[50,3072]{1,0:T(8,128)S(1)}, f32[50,3072]{1,0:T(8,128)}, u32[]{:S(2)}) copy-start(f32[50,3072]{1,0:T(8,128)} %param.21) | copy-start | bytes 1843204
  7.2 207.3 %all-gather.5.cloned.1.call-start = ((), (), s32[]{:S(2)}) async-start(), calls=%async_computation | async-start | bytes 17694720 | tf_op jit(solution)/shard_map/all_gather | solution.py:130
  7.9 248.6 %all-gather.7.cloned.1.call-start = ((), (), s32[]{:S(2)}) async-start(), calls=%async_computation.1 | async-start | bytes 5898240 | tf_op jit(solution)/shard_map/all_gather | solution.py:131
  11.2 39.8 %collective-permute-start.1 = (bf16[256,3072]{1,0:T(8,128)(2,1)}, bf16[256,3072]{1,0:T(8,128)(2,1)}, u32[]{:S(2)}, u32[]{:S(2)}) collective-permute-start(bf16[256,3072]{1,0:T(8,128)(2,1)} %get-tuple-element.59), channel_id=1, source_target_pairs={{0,4},{4,8},{8,12},{12,0},{1,5},{5,9},{9,13},{13,1},{2,6},{6,10},{... | collective-permute-start | bytes 4718600 | tf_op jit(solution)/shard_map/ppermute | solution.py:138
  14.3 19.9 %collective-permute-start = (bf16[256,1536]{1,0:T(8,128)(2,1)S(1)}, bf16[256,1536]{1,0:T(8,128)(2,1)}, u32[]{:S(2)}, u32[]{:S(2)}) collective-permute-start(bf16[256,1536]{1,0:T(8,128)(2,1)S(1)} %slice.155), channel_id=1, source_target_pairs={{0,16},{1,17},{2,18},{3,19},{4,20},{5,21},{6,22},{7,23},{8,24},{9,... | collective-permute-start | bytes 2359304 | tf_op jit(solution)/shard_map/ppermute | solution.py:141
  18.6 20.7 %collective-permute-start.13 = (bf16[256,1536]{1,0:T(8,128)(2,1)S(1)}, bf16[256,1536]{1,0:T(8,128)(2,1)}, u32[]{:S(2)}, u32[]{:S(2)}) collective-permute-start(bf16[256,1536]{1,0:T(8,128)(2,1)S(1)} %slice.155), channel_id=1, source_target_pairs={{16,0},{17,1},{18,2},{19,3},{20,4},{21,5},{22,6},{23,7},{24,8},{25... | collective-permute-start | bytes 2359304 | tf_op jit(solution)/shard_map/ppermute | solution.py:141
  19.9 124.8 %copy-start.16 = (f32[2,1,128,64]{2,3,1,0:T(8,128)S(1)}, f32[2,1,128,64]{2,3,1,0:T(8,128)}, u32[]{:S(2)}) copy-start(f32[2,1,128,64]{2,3,1,0:T(8,128)} %param.13) | copy-start | bytes 196612
  41.4 108.0 %copy-start.18 = (s32[2,4]{1,0:T(2,128)S(1)}, s32[2,4]{1,0:T(2,128)}, u32[]{:S(2)}) copy-start(s32[2,4]{1,0:T(2,128)} %param.14) | copy-start | bytes 100
  41.4 108.3 %copy-start.17 = (bf16[64,1536]{1,0:T(8,128)(2,1)S(1)}, bf16[64,1536]{1,0:T(8,128)(2,1)}, u32[]{:S(2)}) copy-start(bf16[64,1536]{1,0:T(8,128)(2,1)} %param.16) | copy-start | bytes 589828
  51.0 20.5 %collective-permute-start.2 = (bf16[256,1536]{1,0:T(8,128)(2,1)S(1)}, bf16[256,1536]{1,0:T(8,128)(2,1)S(1)}, u32[]{:S(2)}, u32[]{:S(2)}) collective-permute-start(bf16[256,1536]{1,0:T(8,128)(2,1)S(1)} %get-tuple-element.7), channel_id=1, source_target_pairs={{0,4},{4,8},{8,12},{12,0},{1,5},{5,9},{9,13},{13,1},{2,6},{6,10},{... | collective-permute-start | bytes 2359304 | tf_op jit(solution)/shard_map/ppermute | solution.py:138
  71.5 128.0 %copy-start.12 = (bf16[256,1536]{1,0:T(8,128)(2,1)}, bf16[256,1536]{1,0:T(8,128)(2,1)S(1)}, u32[]{:S(2)}) copy-start(bf16[256,1536]{1,0:T(8,128)(2,1)S(1)} %collective-permute-done.2.refs_2_) | copy-start | bytes 2359300
  71.5 19.6 %collective-permute-start.4 = (bf16[256,1536]{1,0:T(8,128)(2,1)S(1)}, bf16[256,1536]{1,0:T(8,128)(2,1)S(1)}, u32[]{:S(2)}, u32[]{:S(2)}) collective-permute-start(bf16[256,1536]{1,0:T(8,128)(2,1)S(1)} %collective-permute-done.2.refs_2_), channel_id=1, source_target_pairs={{0,4},{4,8},{8,12},{12,0},{1,5},{5,9},{9,13},{13,1},{2,6},{6,10},{... | collective-permute-start | bytes 2359304 | tf_op jit(solution)/shard_map/ppermute | solution.py:138
  91.1 0.9 copy-start.13
  91.1 18.8 %collective-permute-start.6 = (bf16[256,1536]{1,0:T(8,128)(2,1)S(1)}, bf16[256,1536]{1,0:T(8,128)(2,1)}, u32[]{:S(2)}, u32[]{:S(2)}) collective-permute-start(bf16[256,1536]{1,0:T(8,128)(2,1)S(1)} %collective-permute-done.4.refs_4_), channel_id=1, source_target_pairs={{0,4},{4,8},{8,12},{12,0},{1,5},{5,9},{9,13},{13,1},{2,6},{6,10},{... | collective-permute-start | bytes 2359304 | tf_op jit(solution)/shard_map/ppermute | solution.py:138
  109.9 34.8 %collective-permute-start.9 = (bf16[256,3072]{1,0:T(8,128)(2,1)}, bf16[256,3072]{1,0:T(8,128)(2,1)S(1)}, u32[]{:S(2)}, u32[]{:S(2)}) collective-permute-start(bf16[256,3072]{1,0:T(8,128)(2,1)} %collective-permute-done.1.refs_2_.refs_3_), channel_id=1, source_target_pairs={{0,4},{4,8},{8,12},{12,0},{1,5},{5,9},{9,13},{13,1},{2,6},{6,10},{... | collective-permute-start | bytes 4718600 | tf_op jit(solution)/shard_map/ppermute | solution.py:138
  144.7 5.6 %copy-start.6 = (bf16[256,3072]{1,0:T(8,128)(2,1)}, bf16[256,3072]{1,0:T(8,128)(2,1)S(1)}, u32[]{:S(2)}) copy-start(bf16[256,3072]{1,0:T(8,128)(2,1)S(1)} %collective-permute-done.9.refs_4_.refs_5_) | copy-start | bytes 4718596
  144.7 34.6 %collective-permute-start.10 = (bf16[256,3072]{1,0:T(8,128)(2,1)S(1)}, bf16[256,3072]{1,0:T(8,128)(2,1)}, u32[]{:S(2)}, u32[]{:S(2)}) collective-permute-start(bf16[256,3072]{1,0:T(8,128)(2,1)S(1)} %collective-permute-done.9.refs_4_.refs_5_), channel_id=1, source_target_pairs={{0,4},{4,8},{8,12},{12,0},{1,5},{5,9},{9,13},{13,1},{2,6},{6,10},{... | collective-permute-start | bytes 4718600 | tf_op jit(solution)/shard_map/ppermute | solution.py:138
  149.7 29.6 %copy-start.15 = (bf16[256,1536]{1,0:T(8,128)(2,1)S(1)}, bf16[256,1536]{1,0:T(8,128)(2,1)}, u32[]{:S(2)}) copy-start(bf16[256,1536]{1,0:T(8,128)(2,1)} %get-tuple-element.9) | copy-start | bytes 2359300
  150.3 29.9 %copy-start.2 = (f32[512,1536]{1,0:T(8,128)}, f32[512,1536]{1,0:T(8,128)S(1)}, u32[]{:S(2)}) copy-start(f32[512,1536]{1,0:T(8,128)S(1)} %fusion.88) | copy-start | bytes 9437188
  150.3 28.9 %copy-start.19 = (f32[1,3072]{1,0:T(1,128)S(1)}, f32[1,3072]{1,0:T(1,128)}, u32[]{:S(2)}) copy-start(f32[1,3072]{1,0:T(1,128)} %param.19) | copy-start | bytes 36868
  150.3 29.0 %copy-start.20 = (s32[2]{0:T(128)S(1)}, s32[2]{0:T(128)}, u32[]{:S(2)}) copy-start(s32[2]{0:T(128)} %param.15) | copy-start | bytes 28
  150.3 29.4 %copy-start.11 = (f32[1,50,4608]{2,0,1:T(1,128)S(1)}, f32[1,50,4608]{2,0,1:T(1,128)}, u32[]{:S(2)}) copy-start(f32[1,50,4608]{2,0,1:T(1,128)} %param.20) | copy-start | bytes 2764804
  179.3 17.5 %collective-permute-start.14 = (bf16[256,1536]{1,0:T(8,128)(2,1)S(1)}, bf16[256,1536]{1,0:T(8,128)(2,1)}, u32[]{:S(2)}, u32[]{:S(2)}) collective-permute-start(bf16[256,1536]{1,0:T(8,128)(2,1)S(1)} %copy-done.15), channel_id=1, source_target_pairs={{0,4},{4,8},{8,12},{12,0},{1,5},{5,9},{9,13},{13,1},{2,6},{6,10},{... | collective-permute-start | bytes 2359304 | tf_op jit(solution)/shard_map/ppermute | solution.py:138
  179.7 21.1 %copy-start.14 = (bf16[256,1536]{1,0:T(8,128)(2,1)S(1)}, bf16[256,1536]{1,0:T(8,128)(2,1)}, u32[]{:S(2)}) copy-start(bf16[256,1536]{1,0:T(8,128)(2,1)} %copy-done.13) | copy-start | bytes 2359300
  196.8 17.7 %collective-permute-start.16 = (bf16[256,1536]{1,0:T(8,128)(2,1)}, bf16[256,1536]{1,0:T(8,128)(2,1)}, u32[]{:S(2)}, u32[]{:S(2)}) collective-permute-start(bf16[256,1536]{1,0:T(8,128)(2,1)} %collective-permute-done.14.refs_2_), channel_id=1, source_target_pairs={{0,4},{4,8},{8,12},{12,0},{1,5},{5,9},{9,13},{13,1},{2,6},{6,10},{... | collective-permute-start | bytes 2359304 | tf_op jit(solution)/shard_map/ppermute | solution.py:138
  199.5 27.4 %collective-permute-start.3 = (bf16[256,1536]{1,0:T(8,128)(2,1)S(1)}, bf16[256,1536]{1,0:T(8,128)(2,1)}, u32[]{:S(2)}, u32[]{:S(2)}) collective-permute-start(bf16[256,1536]{1,0:T(8,128)(2,1)S(1)} %collective-permute-done.2.refs_2_), channel_id=1, source_target_pairs={{16,0},{17,1},{18,2},{19,3},{20,4},{21,5},{22,6},{23,7},{24,8},{25... | collective-permute-start | bytes 2359304 | tf_op jit(solution)/shard_map/ppermute | solution.py:141
  200.8 37.9 %collective-permute-start.5 = (bf16[256,1536]{1,0:T(8,128)(2,1)S(1)}, bf16[256,1536]{1,0:T(8,128)(2,1)}, u32[]{:S(2)}, u32[]{:S(2)}) collective-permute-start(bf16[256,1536]{1,0:T(8,128)(2,1)S(1)} %copy-done.14), channel_id=1, source_target_pairs={{16,0},{17,1},{18,2},{19,3},{20,4},{21,5},{22,6},{23,7},{24,8},{25... | collective-permute-start | bytes 2359304 | tf_op jit(solution)/shard_map/ppermute | solution.py:141
  202.1 45.0 %collective-permute-start.7 = (bf16[256,1536]{1,0:T(8,128)(2,1)}, bf16[256,1536]{1,0:T(8,128)(2,1)}, u32[]{:S(2)}, u32[]{:S(2)}) collective-permute-start(bf16[256,1536]{1,0:T(8,128)(2,1)} %collective-permute-done.6.refs_6_), channel_id=1, source_target_pairs={{16,0},{17,1},{18,2},{19,3},{20,4},{21,5},{22,6},{23,7},{24,8},{25... | collective-permute-start | bytes 2359304 | tf_op jit(solution)/shard_map/ppermute | solution.py:141
  214.5 52.6 %collective-permute-start.18 = (bf16[256,1536]{1,0:T(8,128)(2,1)}, bf16[256,1536]{1,0:T(8,128)(2,1)}, u32[]{:S(2)}, u32[]{:S(2)}) collective-permute-start(bf16[256,1536]{1,0:T(8,128)(2,1)} %collective-permute-done.16.refs_4_), channel_id=1, source_target_pairs={{0,4},{4,8},{8,12},{12,0},{1,5},{5,9},{9,13},{13,1},{2,6},{6,10},{... | collective-permute-start | bytes 2359304 | tf_op jit(solution)/shard_map/ppermute | solution.py:138
  222.2 2.2 copy-start.4
  256.5 24.1 %copy-start.3 = (f32[512,1536]{1,0:T(8,128)S(1)}, f32[512,1536]{1,0:T(8,128)}, u32[]{:S(2)}) copy-start(f32[512,1536]{1,0:T(8,128)} %copy-done.2) | copy-start | bytes 9437188
  261.1 19.4 %collective-permute-start.8 = (bf16[256,1536]{1,0:T(8,128)(2,1)S(1)}, bf16[256,1536]{1,0:T(8,128)(2,1)S(1)}, u32[]{:S(2)}, u32[]{:S(2)}) collective-permute-start(bf16[256,1536]{1,0:T(8,128)(2,1)S(1)} %fusion.30), channel_id=1, source_target_pairs={{0,16},{1,17},{2,18},{3,19},{4,20},{5,21},{6,22},{7,23},{8,24},{9,... | collective-permute-start | bytes 2359304 | tf_op jit(solution)/shard_map/ppermute | solution.py:21
  262.6 87.8 %collective-permute-start.15 = (bf16[256,1536]{1,0:T(8,128)(2,1)}, bf16[256,1536]{1,0:T(8,128)(2,1)}, u32[]{:S(2)}, u32[]{:S(2)}) collective-permute-start(bf16[256,1536]{1,0:T(8,128)(2,1)} %collective-permute-done.14.refs_2_), channel_id=1, source_target_pairs={{0,16},{1,17},{2,18},{3,19},{4,20},{5,21},{6,22},{7,23},{8,24},{9,... | collective-permute-start | bytes 2359304 | tf_op jit(solution)/shard_map/ppermute | solution.py:141
  264.8 85.6 %collective-permute-start.17 = (bf16[256,1536]{1,0:T(8,128)(2,1)}, bf16[256,1536]{1,0:T(8,128)(2,1)}, u32[]{:S(2)}, u32[]{:S(2)}) collective-permute-start(bf16[256,1536]{1,0:T(8,128)(2,1)} %collective-permute-done.16.refs_4_), channel_id=1, source_target_pairs={{0,16},{1,17},{2,18},{3,19},{4,20},{5,21},{6,22},{7,23},{8,24},{9,... | collective-permute-start | bytes 2359304 | tf_op jit(solution)/shard_map/ppermute | solution.py:141
  267.0 83.4 %collective-permute-start.19 = (bf16[256,1536]{1,0:T(8,128)(2,1)}, bf16[256,1536]{1,0:T(8,128)(2,1)}, u32[]{:S(2)}, u32[]{:S(2)}) collective-permute-start(bf16[256,1536]{1,0:T(8,128)(2,1)} %collective-permute-done.18.refs_6_), channel_id=1, source_target_pairs={{0,16},{1,17},{2,18},{3,19},{4,20},{5,21},{6,22},{7,23},{8,24},{9,... | collective-permute-start | bytes 2359304 | tf_op jit(solution)/shard_map/ppermute | solution.py:141
  288.7 2.2 copy-start.5
  307.4 4.8 %copy-start.21 = (bf16[1536,64]{0,1:T(8,128)(2,1)S(1)}, bf16[1536,64]{0,1:T(8,128)(2,1)}, u32[]{:S(2)}) copy-start(bf16[1536,64]{0,1:T(8,128)(2,1)} %param.22) | copy-start | bytes 589828
  307.7 30.9 %collective-permute-start.12 = (bf16[256,1536]{1,0:T(8,128)(2,1)S(1)}, bf16[256,1536]{1,0:T(8,128)(2,1)S(1)}, u32[]{:S(2)}, u32[]{:S(2)}) collective-permute-start(bf16[256,1536]{1,0:T(8,128)(2,1)S(1)} %get-tuple-element.64), channel_id=1, source_target_pairs={{0,16},{1,17},{2,18},{3,19},{4,20},{5,21},{6,22},{7,23},{8,24},{9,... | collective-permute-start | bytes 2359304 | tf_op jit(solution)/shard_map/ppermute | solution.py:21
  312.6 5.6 %collective-permute-start.11 = (bf16[128,64]{0,1:T(8,128)(2,1)S(1)}, bf16[128,64]{0,1:T(8,128)(2,1)S(1)}, u32[]{:S(2)}, u32[]{:S(2)}) collective-permute-start(bf16[128,64]{0,1:T(8,128)(2,1)S(1)} %slice.231), channel_id=1, source_target_pairs={{16,0},{17,1},{18,2},{19,3},{20,4},{21,5},{22,6},{23,7},{24,8},{25... | collective-permute-start | bytes 49160 | tf_op jit(solution)/shard_map/ppermute | solution.py:21
  338.5 8.0 %copy-start.7 = (bf16[256,1536]{1,0:T(8,128)(2,1)}, bf16[256,1536]{1,0:T(8,128)(2,1)S(1)}, u32[]{:S(2)}) copy-start(bf16[256,1536]{1,0:T(8,128)(2,1)S(1)} %collective-permute-done.12) | copy-start | bytes 2359300
  364.1 2.1 copy-start.8
  364.1 2.1 copy-start.9
  364.1 2.1 copy-start.10
  364.9 5.6 %collective-permute-start.20 = (bf16[128,64]{0,1:T(8,128)(2,1)S(1)}, bf16[128,64]{0,1:T(8,128)(2,1)S(1)}, u32[]{:S(2)}, u32[]{:S(2)}) collective-permute-start(bf16[128,64]{0,1:T(8,128)(2,1)S(1)} %slice.230), channel_id=1, source_target_pairs={{16,0},{17,1},{18,2},{19,3},{20,4},{21,5},{22,6},{23,7},{24,8},{25... | collective-permute-start | bytes 49160 | tf_op jit(solution)/shard_map/ppermute | solution.py:21
  367.1 4.8 %copy-start.1 = (f32[50,3072]{1,0:T(8,128)S(1)}, f32[50,3072]{1,0:T(8,128)}, u32[]{:S(2)}) copy-start(f32[50,3072]{1,0:T(8,128)} %param.21) | copy-start | bytes 1843204
Sparse Core Ops, SparseCore 0:
  9.6 93.7 all-gather.4
  110.0 38.1 all-gather.6
